TPU v7x, 256 devices: a whole 4x4x8 slice. The times are simulated.
256 devices in a mesh: grp: 16 (over y, x), leaf: 16 (over z, core).
Axes of the slice: x: 4, y: 4, z: 8, core: 2. Of those that a mesh axis runs over, the one named last changes fastest.
Arguments:
- direction: bfloat16 [393216, 256], P(('grp', 'leaf')), may hold values from -6 to 6
- residual: bfloat16 [393216, 256], P(('grp', 'leaf')), may hold values from -6 to 6
- leaf_order: int32 [256, 1536], P(('grp', 'leaf')), may hold values from 0 to 1535, as said below
- diag_block: bfloat16 [256, 1536, 1536], P(('grp', 'leaf')), may hold values from -0.15625 to 0.15625
- up_basis: bfloat16 [256, 1536, 128], P(('grp', 'leaf')), may hold values from -0.15625 to 0.15625
- down_basis: bfloat16 [256, 1536, 128], P(('grp', 'leaf')), may hold values from -0.5 to 0.5
- leaf_ops: bfloat16 [3, 256, 128, 128], P(None, ('grp', 'leaf')), may hold values from -0.375 to 0.375
- inner_ops: bfloat16 [3, 224, 128, 128], P(None, 'grp'), may hold values from -0.375 to 0.375
- top_ops: bfloat16 [3, 30, 128, 128], replicated, may hold values from -0.375 to 0.375
- ridge_shift: float32 [1], replicated, may hold values from 0.5 to 2
Outputs:
- image: bfloat16 [393216, 256], P(('grp', 'leaf'))
- curvature_gram: float32 [256, 256], replicated
- residual_gram: float32 [256, 256], replicated
Inputs may be any that keep to these rules, and one draw needn't show every extreme that they name: Each row of leaf_order is a permutation of 0 to 1535.
All inputs are finite; a program needn't handle non-finite values.
Results may differ from a plain program's by a relative error of at most 0.022.
Values may be sent and summed in bfloat16 or wider, within the bound.
A program may use at most 64 MiB of HBM per device.

v0:
```python
import jax
import jax.numpy as jnp
from jax import lax
from jax.sharding import Mesh
from jax.sharding import PartitionSpec as P

LEAF = ("leaf_0", "leaf_1")
GRP = ("grp_0", "grp_1")
GRP_LEAF = ("grp_0", "grp_1", "leaf_0", "leaf_1")


def from_partner(block, axis, apart):
    count = lax.axis_size(axis)
    route = []
    for low in range(count):
        high = low | 1 << apart
        if high != low and high < count:
            route += [(low, high), (high, low)]
    return lax.ppermute(block, axis, route)


def cut_along(shard, dim, length):
    before, after = (shard.shape[:dim], shard.shape[dim + 1 :])
    return jnp.moveaxis(shard.reshape(*before, length, -1, *after), dim, 0)


def sum_at_owner(shard, axis, dim):
    length = lax.axis_size(axis)
    pieces = lax.all_to_all(cut_along(shard, dim, length), axis, 0, 0, tiled=True)
    return jnp.sum(pieces, axis=0)


def summed_rows(shard, axes, dim):
    far, near = axes
    pieces = cut_along(shard, dim, lax.axis_size(far))
    nearer = sum_at_owner(pieces, near, dim + 1)
    arrived = lax.all_to_all(nearer, far, split_axis=0, concat_axis=0, tiled=True)
    return arrived.sum(axis=0)


def filled_up(lines, length):
    spare = -lines.shape[0] % length
    if not spare:
        return lines
    return jnp.concatenate([lines, jnp.zeros((spare, *lines.shape[1:]), lines.dtype)])


def copy_for_each(shard, axis):
    copies = jnp.broadcast_to(shard, (lax.axis_size(axis), *shard.shape))
    return lax.all_to_all(copies, axis, split_axis=0, concat_axis=0, tiled=True)


def in_order(pieces, dim):
    shape = list(pieces.shape[1:])
    shape[dim] *= pieces.shape[0]
    return jnp.moveaxis(pieces, 0, dim).reshape(shape)


def gathered_by_axis(shard, axes, dim):
    far, near = axes
    pieces = copy_for_each(copy_for_each(shard, far), near)
    return in_order(pieces.swapaxes(0, 1).reshape(-1, *shard.shape), dim)


def total_of(shard, axes):
    own = summed_rows(filled_up(shard, lax.axis_size(axes[0]) * lax.axis_size(axes[1])), axes, 0)
    whole = gathered_by_axis(own, axes, 0)
    return whole[: len(shard)].reshape(shard.shape)


def together(arrays, axis):
    ends = [0]
    for a in arrays:
        ends.append(ends[-1] + a.size)
    so_far = total_of(jnp.concatenate([a.ravel() for a in arrays]), axis)
    return tuple((so_far[b:e].reshape(a.shape) for a, b, e in zip(arrays, ends, ends[1:])))


def lift_single(transfer, skeleton):
    return jnp.einsum("rs,rk->sk", transfer, skeleton, preferred_element_type=jnp.float32).astype(
        jnp.bfloat16
    )


def body(
    direction,
    residual,
    leaf_order,
    diag_block,
    up_basis,
    down_basis,
    leaf_ops,
    inner_ops,
    top_ops,
    ridge_shift,
):
    leaves_here = lax.axis_size(LEAF)
    groups = lax.axis_size(GRP)
    leaf_levels = leaves_here.bit_length() - 1
    group_levels = groups.bit_length() - 1
    total_levels = leaf_levels + group_levels
    my_leaf = lax.axis_index(LEAF)
    my_group = lax.axis_index(GRP)
    ordering = leaf_order[0]
    ordered = jnp.take(direction, ordering, axis=0)
    skeleton = jnp.einsum(
        "nr,nk->rk", up_basis[0], ordered, preferred_element_type=jnp.float32
    ).astype(jnp.bfloat16)

    def inner_offset(height):
        return sum((leaves_here >> section for section in range(1, height)))

    def top_offset(upper_level):
        return sum((groups >> section for section in range(upper_level)))

    def path_operators(height):
        if height == 0:
            return leaf_ops[:, 0]
        if height < leaf_levels:
            return lax.dynamic_index_in_dim(
                inner_ops, inner_offset(height) + (my_leaf >> height), 1, keepdims=False
            )
        upper_level = height - leaf_levels
        return lax.dynamic_index_in_dim(
            top_ops, top_offset(upper_level) + (my_group >> upper_level), 1, keepdims=False
        )

    contrib = lift_single(leaf_ops[0, 0], skeleton)
    siblings = []
    for bit_index in range(leaf_levels):
        other_skeleton, other_contrib = from_partner((skeleton, contrib), LEAF, bit_index)
        siblings.append(other_skeleton)
        skeleton = (contrib.astype(jnp.float32) + other_contrib.astype(jnp.float32)).astype(
            jnp.bfloat16
        )
        contrib = lift_single(path_operators(bit_index + 1)[0], skeleton)
    for bit_index in range(group_levels):
        other_skeleton, other_contrib = from_partner((skeleton, contrib), GRP, bit_index)
        siblings.append(other_skeleton)
        if bit_index + 1 < group_levels:
            skeleton = (contrib.astype(jnp.float32) + other_contrib.astype(jnp.float32)).astype(
                jnp.bfloat16
            )
            contrib = lift_single(path_operators(leaf_levels + bit_index + 1)[0], skeleton)
    coarse = jnp.zeros((up_basis.shape[2], direction.shape[1]), jnp.bfloat16)
    for height in reversed(range(total_levels)):
        operators = path_operators(height)
        coupled = jnp.dot(operators[2], siblings[height], preferred_element_type=jnp.float32)
        passed = jnp.dot(operators[1], coarse, preferred_element_type=jnp.float32)
        coarse = (coupled + passed).astype(jnp.bfloat16)
    local = jnp.dot(diag_block[0], ordered, preferred_element_type=jnp.float32)
    local = local + jnp.dot(down_basis[0], coarse, preferred_element_type=jnp.float32)
    restored = jnp.zeros(local.shape, jnp.float32).at[ordering].set(local)
    image = (restored + ridge_shift[0] * direction.astype(jnp.float32)).astype(jnp.bfloat16)
    curvature_part = jnp.einsum("nk,nm->km", direction, image, preferred_element_type=jnp.float32)
    correlation_part = jnp.einsum("nk,nm->km", residual, image, preferred_element_type=jnp.float32)
    curvature, correlation = together(
        (curvature_part, correlation_part), ("grp_0", ("grp_1", "leaf_0", "leaf_1"))
    )
    points_total = direction.shape[0] * leaves_here * groups
    return (image, curvature / points_total, correlation / points_total)


def solution(mesh):
    finer = Mesh(mesh.devices.reshape(4, 4, 8, 2), ("grp_0", "grp_1", "leaf_0", "leaf_1"))
    in_specs = (
        P(GRP_LEAF, None),
        P(GRP_LEAF, None),
        P(GRP_LEAF, None),
        P(GRP_LEAF, None, None),
        P(GRP_LEAF, None, None),
        P(GRP_LEAF, None, None),
        P(None, GRP_LEAF, None, None),
        P(None, GRP, None, None),
        P(),
        P(),
    )
    out_specs = (P(GRP_LEAF, None), P(), P())
    return jax.shard_map(body, mesh=finer, in_specs=in_specs, out_specs=out_specs, check_vma=False)
```

profile of v0, /device:TPU:1, one launch (start us, length us, event | category | flops | bytes accessed | tf_op | source)
XLA Modules:
  0.0 177.3 jit_solution(14332516198037152972)
XLA Ops:
  2.3 5.8 %gather_fusion = bf16[1536,256]{1,0:T(8,128)(2,1)} fusion(bf16[1536,256]{1,0:T(8,128)(2,1)} %param.10, s32[2048]{0:T(1024)S(1)} %pad_clamp_fusion), kind=kCustom, calls=%fused_computation | custom fusion | bytes 1579008 | tf_op jit(solution)/shard_map/jit(_take)/gather | solution.py:105
  8.1 2.5 %convolution_convert_fusion = bf16[256,128]{1,0:T(8,128)(2,1)} fusion(bf16[1,1536,128]{2,1,0:T(8,128)(2,1)S(1)} %copy-done.4, bf16[1536,256]{1,0:T(8,128)(2,1)} %gather_fusion, pred[1536]{0:T(1024)(128)(4,1)S(1)} %compare_and_fusion), kind=kOutput, calls=%fused_computation.17 | convolution fusion | flops 101089280 | bytes 1246720 | tf_op jit(solution)/shard_map/nr,nk->rk/dot_general | solution.py:106
  11.5 3.3 %collective-permute-start.1 = (bf16[128,256]{0,1:T(8,128)(2,1)S(1)}, bf16[128,256]{0,1:T(8,128)(2,1)S(1)}, u32[]{:S(2)}, u32[]{:S(2)}) collective-permute-start(bf16[128,256]{0,1:T(8,128)(2,1)S(1)} %fusion.11), channel_id=1, source_target_pairs={{0,1},{1,0},{2,3},{3,2},{4,5},{5,4},{6,7},{7,6},{8,9},{9,8},{10,11... | collective-permute-start | bytes 196616 | tf_op jit(solution)/shard_map/ppermute | solution.py:19
  16.9 3.1 %collective-permute-done.3 = bf16[128,256]{1,0:T(8,128)(2,1)S(1)} collective-permute-done((bf16[128,256]{1,0:T(8,128)(2,1)S(1)}, bf16[128,256]{1,0:T(8,128)(2,1)S(1)}, u32[]{:S(2)}, u32[]{:S(2)}) %collective-permute-start.3) | collective-permute-done | bytes 65568 | tf_op jit(solution)/shard_map/ppermute | solution.py:19
  20.9 1.9 %collective-permute-start.5 = (bf16[128,256]{1,0:T(8,128)(2,1)S(1)}, bf16[128,256]{1,0:T(8,128)(2,1)S(1)}, u32[]{:S(2)}, u32[]{:S(2)}) collective-permute-start(bf16[128,256]{1,0:T(8,128)(2,1)S(1)} %convolution_convert_fusion.5), channel_id=1, source_target_pairs={{0,4},{4,0},{1,5},{5,1},{2,6},{6,2},{3,7},{7,3},{8,12},{12,8},{9,1... | collective-permute-start | bytes 196616 | tf_op jit(solution)/shard_map/ppermute | solution.py:19
  22.9 2.9 %collective-permute-done.5 = bf16[128,256]{1,0:T(8,128)(2,1)S(1)} collective-permute-done((bf16[128,256]{1,0:T(8,128)(2,1)S(1)}, bf16[128,256]{1,0:T(8,128)(2,1)S(1)}, u32[]{:S(2)}, u32[]{:S(2)}) %collective-permute-start.5) | collective-permute-done | bytes 65568 | tf_op jit(solution)/shard_map/ppermute | solution.py:19
  26.7 5.3 %collective-permute-start.7 = (bf16[128,256]{1,0:T(8,128)(2,1)S(1)}, bf16[128,256]{1,0:T(8,128)(2,1)S(1)}, u32[]{:S(2)}, u32[]{:S(2)}) collective-permute-start(bf16[128,256]{1,0:T(8,128)(2,1)S(1)} %convolution_convert_fusion.4), channel_id=1, source_target_pairs={{0,8},{8,0},{1,9},{9,1},{2,10},{10,2},{3,11},{11,3},{4,12},{12,4},... | collective-permute-start | bytes 196616 | tf_op jit(solution)/shard_map/ppermute | solution.py:19
  32.0 1.9 %collective-permute-done.7 = bf16[128,256]{1,0:T(8,128)(2,1)S(1)} collective-permute-done((bf16[128,256]{1,0:T(8,128)(2,1)S(1)}, bf16[128,256]{1,0:T(8,128)(2,1)S(1)}, u32[]{:S(2)}, u32[]{:S(2)}) %collective-permute-start.7) | collective-permute-done | bytes 65568 | tf_op jit(solution)/shard_map/ppermute | solution.py:19
  34.1 1.2 collective-permute-start.9
  35.2 2.3 %collective-permute-done.9 = bf16[128,256]{1,0:T(8,128)(2,1)S(1)} collective-permute-done((bf16[128,256]{1,0:T(8,128)(2,1)S(1)}, bf16[128,256]{1,0:T(8,128)(2,1)S(1)}, u32[]{:S(2)}, u32[]{:S(2)}) %collective-permute-start.9) | collective-permute-done | bytes 65568 | tf_op jit(solution)/shard_map/ppermute | solution.py:19
  37.8 2.4 %collective-permute-start.11 = (bf16[128,256]{1,0:T(8,128)(2,1)S(1)}, bf16[128,256]{1,0:T(8,128)(2,1)S(1)}, u32[]{:S(2)}, u32[]{:S(2)}) collective-permute-start(bf16[128,256]{1,0:T(8,128)(2,1)S(1)} %convolution_convert_fusion.2), channel_id=1, source_target_pairs={{0,32},{32,0},{16,48},{48,16},{64,96},{96,64},{80,112},{112,80},{1... | collective-permute-start | bytes 196616 | tf_op jit(solution)/shard_map/ppermute | solution.py:19
  40.2 5.5 %collective-permute-start = (bf16[128,256]{0,1:T(8,128)(2,1)}, bf16[128,256]{0,1:T(8,128)(2,1)}, u32[]{:S(2)}, u32[]{:S(2)}) collective-permute-start(bf16[128,256]{0,1:T(8,128)(2,1)} %bitcast.3), channel_id=1, source_target_pairs={{0,1},{1,0},{2,3},{3,2},{4,5},{5,4},{6,7},{7,6},{8,9},{9,8},{10,11... | collective-permute-start | bytes 196616 | tf_op jit(solution)/shard_map/ppermute | solution.py:19
  47.4 1.4 collective-permute-start.13
  48.8 5.5 %fusion = f32[256,1536]{1,0:T(8,128)} fusion(bf16[1,1536,1536]{2,1,0:T(8,128)(2,1)} %param.13, bf16[1536,256]{1,0:T(8,128)(2,1)} %gather_fusion, pred[1536]{0:T(1024)(128)(4,1)S(1)} %compare_and_fusion), kind=kOutput, calls=%fused_computation.2 | convolution fusion | flops 1208352768 | bytes 7079424 | tf_op jit(solution)/shard_map/dot_general | solution.py:151
  54.9 2.7 %collective-permute-start.14 = (bf16[128,256]{1,0:T(8,128)(2,1)S(1)}, bf16[128,256]{1,0:T(8,128)(2,1)S(1)}, u32[]{:S(2)}, u32[]{:S(2)}) collective-permute-start(bf16[128,256]{1,0:T(8,128)(2,1)S(1)} %add_convert_fusion.1), channel_id=1, source_target_pairs={{0,128},{128,0},{16,144},{144,16},{32,160},{160,32},{48,176},{176,... | collective-permute-start | bytes 196616 | tf_op jit(solution)/shard_map/ppermute | solution.py:19
  58.2 2.8 %collective-permute-start.4 = (bf16[128,256]{1,0:T(8,128)(2,1)S(1)}, bf16[128,256]{1,0:T(8,128)(2,1)}, u32[]{:S(2)}, u32[]{:S(2)}) collective-permute-start(bf16[128,256]{1,0:T(8,128)(2,1)S(1)} %add_convert_fusion.6), channel_id=1, source_target_pairs={{0,4},{4,0},{1,5},{5,1},{2,6},{6,2},{3,7},{7,3},{8,12},{12,8},{9,1... | collective-permute-start | bytes 196616 | tf_op jit(solution)/shard_map/ppermute | solution.py:19
  61.0 4.2 %collective-permute-start.6 = (bf16[128,256]{1,0:T(8,128)(2,1)S(1)}, bf16[128,256]{1,0:T(8,128)(2,1)}, u32[]{:S(2)}, u32[]{:S(2)}) collective-permute-start(bf16[128,256]{1,0:T(8,128)(2,1)S(1)} %add_convert_fusion.5), channel_id=1, source_target_pairs={{0,8},{8,0},{1,9},{9,1},{2,10},{10,2},{3,11},{11,3},{4,12},{12,4},... | collective-permute-start | bytes 196616 | tf_op jit(solution)/shard_map/ppermute | solution.py:19
  67.0 2.3 %collective-permute-done.12 = bf16[128,256]{1,0:T(8,128)(2,1)} collective-permute-done((bf16[128,256]{1,0:T(8,128)(2,1)}, bf16[128,256]{1,0:T(8,128)(2,1)}, u32[]{:S(2)}, u32[]{:S(2)}) %collective-permute-start.12) | collective-permute-done | bytes 65568 | tf_op jit(solution)/shard_map/ppermute | solution.py:19
  70.5 3.5 %collective-permute-done.10 = bf16[128,256]{1,0:T(8,128)(2,1)} collective-permute-done((bf16[128,256]{1,0:T(8,128)(2,1)S(1)}, bf16[128,256]{1,0:T(8,128)(2,1)}, u32[]{:S(2)}, u32[]{:S(2)}) %collective-permute-start.10) | collective-permute-done | bytes 65568 | tf_op jit(solution)/shard_map/ppermute | solution.py:19
  75.3 1.8 %collective-permute-done.8 = bf16[128,256]{1,0:T(8,128)(2,1)S(1)} collective-permute-done((bf16[128,256]{1,0:T(8,128)(2,1)S(1)}, bf16[128,256]{1,0:T(8,128)(2,1)S(1)}, u32[]{:S(2)}, u32[]{:S(2)}) %collective-permute-start.8) | collective-permute-done | bytes 65568 | tf_op jit(solution)/shard_map/ppermute | solution.py:19
  78.2 1.2 fusion.16
  79.4 1.2 fusion.17
  80.6 1.2 fusion.18
  81.8 3.2 %fusion.2 = f32[1536,256]{0,1:T(8,128)} fusion(f32[256,1536]{1,0:T(8,128)} %fusion, f32[256,128]{1,0:T(8,128)S(1)} %fusion.18, bf16[128,256]{0,1:T(8,128)(2,1)} %collective-permute-done, bf16[1,1536,128]{2,1,0:T(8,128)(2,1)} %param.15, bf16[3,1,128,128]{3,2,1,0:T(8,128)(2,1)} %param.16), kind=kOutput, calls=%fused_computation.5 | convolution fusion | flops 109510656 | bytes 3768320 | tf_op jit(solution)/shard_map/dot_general | solution.py:152
  85.1 3.0 %copy.27 = f32[1536,256]{1,0:T(8,128)} copy(f32[1536,256]{0,1:T(8,128)} %fusion.2) | data formatting | bytes 3145728 | tf_op jit(solution)/shard_map/add | solution.py:152
  88.1 8.6 %scatter_custom_fusion = f32[1536,256]{1,0:T(8,128)} fusion(s32[1536]{0:T(1024)S(1)} %fusion.33, f32[1536,256]{1,0:T(8,128)} %copy.27, f32[]{:T(128)} %constant.78.clone.1), kind=kCustom, calls=%fused_computation.41 | custom fusion | bytes 1573376 | tf_op jit(solution)/shard_map/scatter | solution.py:153
  96.7 1.9 %add_convert_fusion = bf16[1536,256]{1,0:T(8,128)(2,1)S(1)} fusion(f32[1536,256]{1,0:T(8,128)} %scatter_custom_fusion, bf16[1536,256]{1,0:T(8,128)(2,1)} %param.10, f32[]{:T(128)} %bitcast.125), kind=kLoop, calls=%fused_computation.6 | loop fusion | flops 1572864 | bytes 3145732 | tf_op jit(solution)/shard_map/convert_element_type | solution.py:154
  100.0 2.5 %convolution_bitcast_fusion = f32[256,256]{0,1:T(8,128)} fusion(bf16[1536,256]{1,0:T(8,128)(2,1)} %copy-done.2, bf16[1536,256]{1,0:T(8,128)(2,1)} %param.11), kind=kOutput, calls=%fused_computation.7 | convolution fusion | flops 201326592 | bytes 1835008 | tf_op jit(solution)/shard_map/nk,nm->km/dot_general | solution.py:156
  105.7 30.9 %all_to_all.28 = f32[64,4,512]{2,1,0:T(4,128)S(1)} all-to-all(f32[64,4,512]{2,1,0:T(4,128)S(1)} %copy.30), channel_id=1, replica_groups=mesh['grp_0'=4,'grp_1'=4,'leaf_0'=8,'leaf_1'=2] {'grp_1','leaf_0','leaf_1'}, dimensions={0} | all-to-all | bytes 1048576 | tf_op jit(solution)/shard_map/all_to_all | solution.py:29
  136.7 6.5 %all_to_all.29 = f32[4,1,512]{2,1,0:T(1,128)S(1)} all-to-all(f32[4,1,512]{2,1,0:T(1,128)S(1)} %all_to_all.19), channel_id=1, replica_groups=mesh['grp_0'=4,'grp_1'=4,'leaf_0'=8,'leaf_1'=2] {'grp_0'}, dimensions={0} | all-to-all | bytes 16384 | tf_op jit(solution)/shard_map/all_to_all | solution.py:37
  143.3 6.5 %all_to_all.30 = f32[4,1,512]{2,1,0:T(1,128)S(1)} all-to-all(f32[4,1,512]{2,1,0:T(1,128)S(1)} %broadcast_in_dim.27), channel_id=1, replica_groups=mesh['grp_0'=4,'grp_1'=4,'leaf_0'=8,'leaf_1'=2] {'grp_0'}, dimensions={0} | all-to-all | bytes 16384 | tf_op jit(solution)/shard_map/all_to_all | solution.py:50
  149.9 25.7 %all_to_all.31 = f32[64,4,512]{2,1,0:T(4,128)S(1)} all-to-all(f32[64,4,512]{2,1,0:T(4,128)S(1)} %broadcast_in_dim.28), channel_id=1, replica_groups=mesh['grp_0'=4,'grp_1'=4,'leaf_0'=8,'leaf_1'=2] {'grp_1','leaf_0','leaf_1'}, dimensions={0} | all-to-all | bytes 1048576 | tf_op jit(solution)/shard_map/all_to_all | solution.py:50
  (63 shorter events, 21.3 us)
Async XLA Ops:
  0.6 33.2 %copy-start = (bf16[3,30,128,128]{3,2,1,0:T(8,128)(2,1)S(1)}, bf16[3,30,128,128]{3,2,1,0:T(8,128)(2,1)}, u32[]{:S(2)}) copy-start(bf16[3,30,128,128]{3,2,1,0:T(8,128)(2,1)} %param.18) | copy-start | bytes 8847364
  2.3 5.8 %copy-start.4 = (bf16[1,1536,128]{2,1,0:T(8,128)(2,1)S(1)}, bf16[1,1536,128]{2,1,0:T(8,128)(2,1)}, u32[]{:S(2)}) copy-start(bf16[1,1536,128]{2,1,0:T(8,128)(2,1)} %param.14) | copy-start | bytes 1179652
  11.5 4.2 %collective-permute-start.1 = (bf16[128,256]{0,1:T(8,128)(2,1)S(1)}, bf16[128,256]{0,1:T(8,128)(2,1)S(1)}, u32[]{:S(2)}, u32[]{:S(2)}) collective-permute-start(bf16[128,256]{0,1:T(8,128)(2,1)S(1)} %fusion.11), channel_id=1, source_target_pairs={{0,1},{1,0},{2,3},{3,2},{4,5},{5,4},{6,7},{7,6},{8,9},{9,8},{10,11... | collective-permute-start | bytes 196616 | tf_op jit(solution)/shard_map/ppermute | solution.py:19
  16.8 3.2 %collective-permute-start.3 = (bf16[128,256]{1,0:T(8,128)(2,1)S(1)}, bf16[128,256]{1,0:T(8,128)(2,1)S(1)}, u32[]{:S(2)}, u32[]{:S(2)}) collective-permute-start(bf16[128,256]{1,0:T(8,128)(2,1)S(1)} %convolution_convert_fusion.6), channel_id=1, source_target_pairs={{0,2},{2,0},{1,3},{3,1},{4,6},{6,4},{5,7},{7,5},{8,10},{10,8},{9,1... | collective-permute-start | bytes 196616 | tf_op jit(solution)/shard_map/ppermute | solution.py:19
  20.9 4.8 %collective-permute-start.5 = (bf16[128,256]{1,0:T(8,128)(2,1)S(1)}, bf16[128,256]{1,0:T(8,128)(2,1)S(1)}, u32[]{:S(2)}, u32[]{:S(2)}) collective-permute-start(bf16[128,256]{1,0:T(8,128)(2,1)S(1)} %convolution_convert_fusion.5), channel_id=1, source_target_pairs={{0,4},{4,0},{1,5},{5,1},{2,6},{6,2},{3,7},{7,3},{8,12},{12,8},{9,1... | collective-permute-start | bytes 196616 | tf_op jit(solution)/shard_map/ppermute | solution.py:19
  26.7 7.1 %collective-permute-start.7 = (bf16[128,256]{1,0:T(8,128)(2,1)S(1)}, bf16[128,256]{1,0:T(8,128)(2,1)S(1)}, u32[]{:S(2)}, u32[]{:S(2)}) collective-permute-start(bf16[128,256]{1,0:T(8,128)(2,1)S(1)} %convolution_convert_fusion.4), channel_id=1, source_target_pairs={{0,8},{8,0},{1,9},{9,1},{2,10},{10,2},{3,11},{11,3},{4,12},{12,4},... | collective-permute-start | bytes 196616 | tf_op jit(solution)/shard_map/ppermute | solution.py:19
  34.1 3.5 %collective-permute-start.9 = (bf16[128,256]{1,0:T(8,128)(2,1)S(1)}, bf16[128,256]{1,0:T(8,128)(2,1)S(1)}, u32[]{:S(2)}, u32[]{:S(2)}) collective-permute-start(bf16[128,256]{1,0:T(8,128)(2,1)S(1)} %convolution_convert_fusion.3), channel_id=1, source_target_pairs={{0,16},{16,0},{32,48},{48,32},{64,80},{80,64},{96,112},{112,96},{1... | collective-permute-start | bytes 196616 | tf_op jit(solution)/shard_map/ppermute | solution.py:19
  37.8 7.9 %collective-permute-start.11 = (bf16[128,256]{1,0:T(8,128)(2,1)S(1)}, bf16[128,256]{1,0:T(8,128)(2,1)S(1)}, u32[]{:S(2)}, u32[]{:S(2)}) collective-permute-start(bf16[128,256]{1,0:T(8,128)(2,1)S(1)} %convolution_convert_fusion.2), channel_id=1, source_target_pairs={{0,32},{32,0},{16,48},{48,16},{64,96},{96,64},{80,112},{112,80},{1... | collective-permute-start | bytes 196616 | tf_op jit(solution)/shard_map/ppermute | solution.py:19
  40.2 41.6 %collective-permute-start = (bf16[128,256]{0,1:T(8,128)(2,1)}, bf16[128,256]{0,1:T(8,128)(2,1)}, u32[]{:S(2)}, u32[]{:S(2)}) collective-permute-start(bf16[128,256]{0,1:T(8,128)(2,1)} %bitcast.3), channel_id=1, source_target_pairs={{0,1},{1,0},{2,3},{3,2},{4,5},{5,4},{6,7},{7,6},{8,9},{9,8},{10,11... | collective-permute-start | bytes 196616 | tf_op jit(solution)/shard_map/ppermute | solution.py:19
  47.4 7.5 %collective-permute-start.13 = (bf16[128,256]{1,0:T(8,128)(2,1)S(1)}, bf16[128,256]{1,0:T(8,128)(2,1)S(1)}, u32[]{:S(2)}, u32[]{:S(2)}) collective-permute-start(bf16[128,256]{1,0:T(8,128)(2,1)S(1)} %convolution_convert_fusion.1), channel_id=1, source_target_pairs={{0,64},{64,0},{16,80},{80,16},{32,96},{96,32},{48,112},{112,48},{1... | collective-permute-start | bytes 196616 | tf_op jit(solution)/shard_map/ppermute | solution.py:19
  54.9 10.2 %collective-permute-start.14 = (bf16[128,256]{1,0:T(8,128)(2,1)S(1)}, bf16[128,256]{1,0:T(8,128)(2,1)S(1)}, u32[]{:S(2)}, u32[]{:S(2)}) collective-permute-start(bf16[128,256]{1,0:T(8,128)(2,1)S(1)} %add_convert_fusion.1), channel_id=1, source_target_pairs={{0,128},{128,0},{16,144},{144,16},{32,160},{160,32},{48,176},{176,... | collective-permute-start | bytes 196616 | tf_op jit(solution)/shard_map/ppermute | solution.py:19
  57.8 22.8 %collective-permute-start.2 = (bf16[128,256]{0,1:T(8,128)(2,1)S(1)}, bf16[128,256]{0,1:T(8,128)(2,1)}, u32[]{:S(2)}, u32[]{:S(2)}) collective-permute-start(bf16[128,256]{0,1:T(8,128)(2,1)S(1)} %add_convert_fusion.7), channel_id=1, source_target_pairs={{0,2},{2,0},{1,3},{3,1},{4,6},{6,4},{5,7},{7,5},{8,10},{10,8},{9,1... | collective-permute-start | bytes 196616 | tf_op jit(solution)/shard_map/ppermute | solution.py:19
  58.2 21.1 %collective-permute-start.4 = (bf16[128,256]{1,0:T(8,128)(2,1)S(1)}, bf16[128,256]{1,0:T(8,128)(2,1)}, u32[]{:S(2)}, u32[]{:S(2)}) collective-permute-start(bf16[128,256]{1,0:T(8,128)(2,1)S(1)} %add_convert_fusion.6), channel_id=1, source_target_pairs={{0,4},{4,0},{1,5},{5,1},{2,6},{6,2},{3,7},{7,3},{8,12},{12,8},{9,1... | collective-permute-start | bytes 196616 | tf_op jit(solution)/shard_map/ppermute | solution.py:19
  61.0 17.1 %collective-permute-start.6 = (bf16[128,256]{1,0:T(8,128)(2,1)S(1)}, bf16[128,256]{1,0:T(8,128)(2,1)}, u32[]{:S(2)}, u32[]{:S(2)}) collective-permute-start(bf16[128,256]{1,0:T(8,128)(2,1)S(1)} %add_convert_fusion.5), channel_id=1, source_target_pairs={{0,8},{8,0},{1,9},{9,1},{2,10},{10,2},{3,11},{11,3},{4,12},{12,4},... | collective-permute-start | bytes 196616 | tf_op jit(solution)/shard_map/ppermute | solution.py:19
  65.2 0.6 copy-start.3
  65.8 3.4 %collective-permute-start.12 = (bf16[128,256]{1,0:T(8,128)(2,1)}, bf16[128,256]{1,0:T(8,128)(2,1)}, u32[]{:S(2)}, u32[]{:S(2)}) collective-permute-start(bf16[128,256]{1,0:T(8,128)(2,1)} %add_convert_fusion.2), channel_id=1, source_target_pairs={{0,64},{64,0},{16,80},{80,16},{32,96},{96,32},{48,112},{112,48},{1... | collective-permute-start | bytes 196616 | tf_op jit(solution)/shard_map/ppermute | solution.py:19
  69.2 4.7 %collective-permute-start.10 = (bf16[128,256]{1,0:T(8,128)(2,1)S(1)}, bf16[128,256]{1,0:T(8,128)(2,1)}, u32[]{:S(2)}, u32[]{:S(2)}) collective-permute-start(bf16[128,256]{1,0:T(8,128)(2,1)S(1)} %add_convert_fusion.3), channel_id=1, source_target_pairs={{0,32},{32,0},{16,48},{48,16},{64,96},{96,64},{80,112},{112,80},{1... | collective-permute-start | bytes 196616 | tf_op jit(solution)/shard_map/ppermute | solution.py:19
  74.0 3.1 %collective-permute-start.8 = (bf16[128,256]{1,0:T(8,128)(2,1)S(1)}, bf16[128,256]{1,0:T(8,128)(2,1)S(1)}, u32[]{:S(2)}, u32[]{:S(2)}) collective-permute-start(bf16[128,256]{1,0:T(8,128)(2,1)S(1)} %add_convert_fusion.4), channel_id=1, source_target_pairs={{0,16},{16,0},{32,48},{48,32},{64,80},{80,64},{96,112},{112,96},{1... | collective-permute-start | bytes 196616 | tf_op jit(solution)/shard_map/ppermute | solution.py:19
  96.7 2.8 %copy-start.1 = (bf16[1536,256]{1,0:T(8,128)(2,1)S(1)}, bf16[1536,256]{1,0:T(8,128)(2,1)}, u32[]{:S(2)}) copy-start(bf16[1536,256]{1,0:T(8,128)(2,1)} %param.10) | copy-start | bytes 2359300
  98.5 0.9 copy-start.2
where the time goes:
time: 178 us; the launch traced here: 177 us
  blocking collectives  69.6 us (39%)
  starting transfers between devices  31.4 us (18%)
  matrix products  27.6 us (16%)
  local copies, waits for them, and re-layouts  23.1 us (13%)
  waiting for transfers between devices  18.6 us (10%)
  other arithmetic  5.4 us (3%)
    all_to_all x2, blocking collectives, copy_for_each(): return lax.all_to_all(copies, axis, split_axis=0, concat_axis=0, tiled=True)  32.2 us
    ppermute x15, starting transfers between devices, from_partner(): return lax.ppermute(block, axis, route)  31.4 us
    all_to_all x1, blocking collectives, sum_at_owner(): lax.all_to_all(cut_along(shard, dim, length), axis, 0, 0, tiled=True)  30.9 us
    ppermute x15, waiting for transfers between devices, from_partner(): return lax.ppermute(block, axis, route)  18.6 us
    scatter x1, local copies, waits for them, and re-layouts, body(): restored = jnp.zeros(local.shape, jnp.float32).at[ordering].set(local)  8.56 us
    dot_general x8, matrix products, body(): passed = jnp.dot(operators[1], coarse, preferred_element_type=jnp.float32)  8.23 us
    all_to_all x1, blocking collectives, summed_rows(): lax.all_to_all(nearer, far, split_axis=0, concat_axis=0, tiled=True)  6.51 us
    gather x1, local copies, waits for them, and re-layouts, body(): ordered = jnp.take(direction, ordering, axis=0)  5.81 us
  transfers between devices with their start and end apart: 15, of which 8 were waited for; matrix products, arithmetic and copies ran while one was open for 9% of the time, Pallas kernels for 0%

commit v1 on v0

v1 whole, which is shorter than its diff:
```python
import jax
import jax.numpy as jnp
from jax import lax
from jax.experimental import pallas as pl
from jax.experimental.pallas import tpu as pltpu
from jax.sharding import PartitionSpec as P

F32 = jnp.float32
BF16 = jnp.bfloat16
GRP_LEAF = ("grp", "leaf")
N = 1536
R = 128
K = 256
D = 16
C = K // D


def mm(a, b):
    return lax.dot_general(a, b, (((1,), (0,)), ((), ())), preferred_element_type=F32)


def mmt(a, b):
    return lax.dot_general(a, b, (((1,), (1,)), ((), ())), preferred_element_type=F32)


def kernel(
    x_h, res_h, ord_h, diag_h, up_h, dn_h, lop_h, iop_h, top_h, ridge_s,
    img_h, cur_h, cor_h,
    x_v, res_v, ord_v, diag_v, up_v, dn_v, lop_v, iop_v, top_v,
    p_v, pt_v, og_v, xt_v, loc_v, im_v, img_v,
    s0_v, sib_v, l1_v, a_r, root_v, b_r, t_v, q_v, vr_v, c_v, c_r,
    gs_v, gs_r, own_v, h_v, h_r, z_v, z_r, f_v, f_r, o_r, out_v,
    load_sem, pair_s, pair_r, a_ss, a_rs, b_ss, b_rs, c_ss, c_rs,
    h_ss, h_rs, z_ss, z_rs, f_ss, f_rs, o_ss, o_rs, store_sem,
):
    me = lax.axis_index("leaf")
    g = lax.axis_index("grp")
    core = lax.rem(me, 2)
    z = me // 2
    sibling = me + 1 - 2 * core

    def other(base, r):
        return lax.rem(base + r, D)

    def sib_of(a):
        return a + 1 - 2 * lax.rem(a, 2)

    def to_leaf(src, dst, ss, rs, j):
        return pltpu.make_async_remote_copy(
            src_ref=src, dst_ref=dst, send_sem=ss, recv_sem=rs,
            device_id={"leaf": j}, device_id_type=pl.DeviceIdType.MESH)

    def to_grp(src, dst, ss, rs, j):
        return pltpu.make_async_remote_copy(
            src_ref=src, dst_ref=dst, send_sem=ss, recv_sem=rs,
            device_id={"grp": j}, device_id_type=pl.DeviceIdType.MESH)

    loads = [
        pltpu.make_async_copy(src, dst, load_sem.at[i])
        for i, (src, dst) in enumerate([
            (ord_h, ord_v), (up_h.at[0], up_v), (lop_h.at[:, 0], lop_v), (x_h, x_v),
            (iop_h, iop_v), (top_h, top_v), (diag_h.at[0], diag_v), (res_h, res_v), (dn_h.at[0], dn_v)])
    ]
    for copy in loads:
        copy.start()
    l_ord, l_up, l_lop, l_x, l_iop, l_top, l_diag, l_res, l_dn = loads

    barrier = pltpu.get_barrier_semaphore()
    for r in range(1, D):
        pl.semaphore_signal(barrier, inc=1, device_id={"leaf": other(me, r)}, device_id_type=pl.DeviceIdType.MESH)
        pl.semaphore_signal(barrier, inc=1, device_id={"grp": other(g, r)}, device_id_type=pl.DeviceIdType.MESH)

    l_ord.wait()
    order = ord_v[...]
    column = jnp.broadcast_to(order.astype(F32), (R, N)).T.astype(jnp.int32)
    lane = lax.broadcasted_iota(jnp.int32, (N, R), 1)
    low = jnp.where((column & (R - 1)) == lane, 1.0, 0.0).astype(BF16)
    high = (column >> 7).astype(BF16)
    for j in range(N // R):
        p_v[:, j * R:(j + 1) * R] = jnp.where(high == jnp.asarray(j, BF16), low, jnp.zeros_like(low))

    l_up.wait()
    l_lop.wait()
    up_t = up_v[...].T
    lift_t = lax.dot_general(lop_v[0], up_t, (((0,), (0,)), ((), ())), preferred_element_type=F32).astype(BF16)
    both_t = jnp.concatenate([up_t, lift_t], axis=0)

    l_x.wait()
    for t in range(3):
        rows = pl.ds(t * 512, 512)
        og_v[rows, :] = mm(p_v[rows, :], x_v[...]).astype(BF16)
    both = mm(both_t, og_v[...]).T
    s0_v[...] = both[:, :R].astype(BF16)
    l1_v[...] = both[:, R:].astype(BF16).reshape(D, C, R)

    pl.semaphore_wait(barrier, 2 * (D - 1))

    sends_a = []
    for r in range(1, D):
        j = other(me, r)
        copy = to_leaf(l1_v.at[j], a_r.at[me], a_ss.at[r], a_rs.at[me], j)
        copy.start()
        sends_a.append(copy)
    pair = to_leaf(s0_v, sib_v, pair_s.at[0], pair_r.at[0], sibling)
    pair.start()
    a_r[me] = l1_v[me]

    l_iop.wait()
    l_top.wait()
    up2 = [mm(iop_v[0, 8 + 2 * m:10 + 2 * m].reshape(2 * R, R), iop_v[0, 12 + m]).astype(BF16) for m in range(2)]
    up1 = [mm(iop_v[0, 2 * m:2 * m + 2].reshape(2 * R, R), up2[m // 2][(m % 2) * R:(m % 2 + 1) * R]).astype(BF16)
           for m in range(4)]

    for r in range(1, D):
        j = other(me, r)
        to_leaf(l1_v.at[j], a_r.at[j], a_ss.at[r], a_rs.at[j], j).wait_recv()
    s1 = [(a_r[2 * m].astype(F32) + a_r[2 * m + 1].astype(F32)).astype(BF16) for m in range(8)]
    s1p = [jnp.concatenate(s1[2 * m:2 * m + 2], axis=1) for m in range(4)]
    root = mm(s1p[0], up1[0])
    for m in range(1, 4):
        root = root + mm(s1p[m], up1[m])
    root_v[...] = root.astype(BF16)

    sends_b = []
    for r in range(1, D):
        j = other(g, r)
        copy = to_grp(root_v, b_r.at[g], b_ss.at[r], b_rs.at[g], j)
        copy.start()
        sends_b.append(copy)
    b_r[g] = root_v[...]

    s2 = [mm(s1p[m], iop_v[0, 2 * m:2 * m + 2].reshape(2 * R, R)).astype(BF16) for m in range(4)]
    s2p = [jnp.concatenate(s2[2 * m:2 * m + 2], axis=1) for m in range(2)]
    s3 = [mm(s2p[m], iop_v[0, 8 + 2 * m:10 + 2 * m].reshape(2 * R, R)).astype(BF16) for m in range(2)]
    c3 = [mmt(s3[1 - m], iop_v[2, 12 + m]).astype(BF16) for m in range(2)]
    c2 = [(mmt(s2[m ^ 1], iop_v[2, 8 + m]) + mmt(c3[m // 2], iop_v[1, 8 + m])).astype(BF16) for m in range(4)]
    c1 = [mmt(s1[m ^ 1], iop_v[2, m]) + mmt(c2[m // 2], iop_v[1, m]) for m in range(8)]
    q2 = [mm(iop_v[1, 8 + m], iop_v[1, 12 + m // 2]).astype(BF16) for m in range(4)]
    for m in range(8):
        q_v[m] = mm(iop_v[1, m], q2[m // 2]).astype(BF16)

    a4, a5, a6, a7 = g, g // 2, g // 4, g // 8
    y5 = top_v[1, a4]
    y6 = mm(y5, top_v[1, 16 + a5]).astype(BF16)
    y7 = mm(y6, top_v[1, 24 + a6]).astype(BF16)
    x5 = mm(y5, top_v[2, 16 + a5]).astype(BF16)
    x6 = mm(y6, top_v[2, 24 + a6]).astype(BF16)
    x7 = mm(y7, top_v[2, 28 + a7]).astype(BF16)

    def lifts(base, node, count):
        return top_v[0, pl.ds(base + node, count)].reshape(count * R, R)

    t_v[g] = jnp.zeros((R, R), BF16)
    n4, n5, n6, n7 = sib_of(a4), sib_of(a5), sib_of(a6), sib_of(a7)
    t_v[n4] = top_v[2, a4].T
    t_v[pl.ds(2 * n5, 2)] = mmt(lifts(0, 2 * n5, 2), x5).astype(BF16).reshape(2, R, R)
    w = mmt(lifts(16, 2 * n6, 2), x6).astype(BF16)
    for b in range(2):
        t_v[pl.ds(4 * n6 + 2 * b, 2)] = mm(lifts(0, 4 * n6 + 2 * b, 2), w[b * R:(b + 1) * R]).astype(BF16).reshape(2, R, R)
    w = mmt(lifts(24, 2 * n7, 2), x7).astype(BF16)
    for b in range(2):
        u = mm(lifts(16, 4 * n7 + 2 * b, 2), w[b * R:(b + 1) * R]).astype(BF16)
        for d in range(2):
            first = 8 * n7 + 4 * b + 2 * d
            t_v[pl.ds(first, 2)] = mm(lifts(0, first, 2), u[d * R:(d + 1) * R]).astype(BF16).reshape(2, R, R)

    for r in range(1, D):
        j = other(g, r)
        to_grp(root_v, b_r.at[j], b_ss.at[r], b_rs.at[j], j).wait_recv()
    c4 = jnp.zeros((C, R), F32)
    for m in range(D // 2):
        c4 = c4 + mm(jnp.concatenate([b_r[2 * m], b_r[2 * m + 1]], axis=1), t_v[2 * m:2 * m + 2].reshape(2 * R, R))
    c4 = c4.astype(BF16)
    for m in range(8):
        c_v[m] = (c1[m] + mmt(c4, q_v[m])).astype(BF16)

    sends_c = []
    for r in range(1, D):
        j = other(me, r)
        copy = to_leaf(c_v.at[j // 2], c_r.at[me], c_ss.at[r], c_rs.at[me], j)
        copy.start()
        sends_c.append(copy)
    c_r[me] = c_v[z]

    l_diag.wait()
    ridge = ridge_s[0]
    for t in range(3):
        rows = pl.ds(t * 512, 512)
        loc_v[rows, :] = mm(diag_v[rows, :], og_v[...]) + ridge * og_v[rows, :].astype(F32)
    l_res.wait()
    xt_v[:K, :] = og_v[...].T
    for t in range(3):
        rows = pl.ds(t * 512, 512)
        xt_v[K:, rows] = mm(p_v[rows, :], res_v[...]).astype(BF16).T
    l_dn.wait()
    vr_v[...] = mm(dn_v[...], lop_v[1]).astype(BF16)
    pair.wait_recv()
    near = mmt(sib_v[...], lop_v[2]).astype(BF16)
    loc_v[...] = loc_v[...] + mmt(dn_v[...], near)
    row = order
    row_low = jnp.broadcast_to(row & (R - 1), (R, N))
    row_high = jnp.broadcast_to(row >> 7, (R, N)).astype(F32).astype(BF16)
    row_one = jnp.where(row_low == lax.broadcasted_iota(jnp.int32, (R, N), 0), 1.0, 0.0).astype(BF16)
    for j in range(N // R):
        pt_v[j * R:(j + 1) * R, :] = jnp.where(row_high == jnp.asarray(j, BF16), row_one, jnp.zeros_like(row_one))

    for r in range(1, D):
        j = other(me, r)
        to_leaf(c_v.at[j // 2], c_r.at[j], c_ss.at[r], c_rs.at[j], j).wait_recv()
    im_v[...] = (loc_v[...] + mmt(vr_v[...], c_r[...].reshape(K, R))).astype(BF16)

    gs_v[...] = mm(xt_v[pl.ds((1 - core) * K, K), :], im_v[...]).astype(BF16)
    swap = to_leaf(gs_v, gs_r, pair_s.at[1], pair_r.at[1], sibling)
    swap.start()
    own_v[...] = mm(xt_v[pl.ds(core * K, K), :], im_v[...])
    swap.wait_recv()
    h_v[...] = (own_v[...] + gs_r[...].astype(F32)).astype(BF16).reshape(D, C, K)
    sends_h = []
    for r in range(1, D):
        j = other(g, r)
        copy = to_grp(h_v.at[j], h_r.at[g], h_ss.at[r], h_rs.at[g], j)
        copy.start()
        sends_h.append(copy)
    h_r[g] = h_v[g]

    stores = []
    for t in range(3):
        rows = pl.ds(t * 512, 512)
        img_v[rows, :] = mm(pt_v[rows, :], im_v[...]).astype(BF16)
        copy = pltpu.make_async_copy(img_v.at[rows], img_h.at[rows], store_sem.at[t])
        copy.start()
        stores.append(copy)

    for r in range(1, D):
        j = other(g, r)
        to_grp(h_v.at[j], h_r.at[j], h_ss.at[r], h_rs.at[j], j).wait_recv()
    total = h_r[0].astype(F32)
    for j in range(1, D):
        total = total + h_r[j].astype(F32)
    z_v[...] = total.astype(BF16)
    sends_z = []
    for r in range(1, D // 2):
        j = lax.rem(me + 2 * r, D)
        copy = to_leaf(z_v, z_r.at[z], z_ss.at[r], z_rs.at[z], j)
        copy.start()
        sends_z.append(copy)
    z_r[z] = z_v[...]
    for r in range(1, D // 2):
        j = lax.rem(me + 2 * r, D)
        to_leaf(z_v, z_r.at[j // 2], z_ss.at[r], z_rs.at[j // 2], j).wait_recv()
    total = z_r[0].astype(F32)
    for j in range(1, D // 2):
        total = total + z_r[j].astype(F32)
    f_v[...] = total.astype(BF16)
    sends_f = []
    for r in range(1, D):
        j = other(g, r)
        copy = to_grp(f_v, f_r.at[g], f_ss.at[r], f_rs.at[g], j)
        copy.start()
        sends_f.append(copy)
    f_r[g] = f_v[...]
    for r in range(D):
        j = other(g, r)
        if r:
            to_grp(f_v, f_r.at[j], f_ss.at[r], f_rs.at[j], j).wait_recv()
        copy = to_leaf(f_r.at[j], o_r.at[j], o_ss.at[j], o_rs.at[j], sibling)
        copy.start()
        sends_f.append(copy)
    scale = 1.0 / (N * D * D)
    out_v[core] = f_r[...].reshape(K, K).astype(F32) * scale
    for j in range(D):
        to_leaf(f_r.at[j], o_r.at[j], o_ss.at[j], o_rs.at[j], sibling).wait_recv()
    out_v[1 - core] = o_r[...].reshape(K, K).astype(F32) * scale
    for i, dst in enumerate((cur_h, cor_h)):
        copy = pltpu.make_async_copy(out_v.at[i], dst, store_sem.at[3 + i])
        copy.start()
        stores.append(copy)

    for copy in [pair, swap, *sends_a, *sends_b, *sends_c, *sends_h, *sends_z, *sends_f]:
        copy.wait_send()
    for copy in stores:
        copy.wait()


def body(*args):
    any_spec = pl.BlockSpec(memory_space=pl.ANY)
    dma = pltpu.SemaphoreType.DMA
    v = pltpu.VMEM
    scratch = [
        v((N, K), BF16), v((N, K), BF16), v((1, N), jnp.int32), v((N, N), BF16), v((N, R), BF16), v((N, R), BF16),
        v((3, R, R), BF16), v((3, 14, R, R), BF16), v((3, 30, R, R), BF16),
        v((N, N), BF16), v((N, N), BF16), v((N, K), BF16), v((2 * K, N), BF16), v((N, K), F32), v((N, K), BF16), v((N, K), BF16),
        v((K, R), BF16), v((K, R), BF16), v((D, C, R), BF16), v((D, C, R), BF16), v((C, R), BF16), v((D, C, R), BF16),
        v((D, R, R), BF16), v((8, R, R), BF16), v((N, R), BF16), v((8, C, R), BF16), v((D, C, R), BF16),
        v((K, K), BF16), v((K, K), BF16), v((K, K), F32), v((D, C, K), BF16), v((D, C, K), BF16), v((C, K), BF16),
        v((8, C, K), BF16), v((C, K), BF16), v((D, C, K), BF16), v((D, C, K), BF16), v((2, K, K), F32),
        dma((9,)), dma((2,)), dma((2,)), *[dma((D,))] * 6, dma((D,)), dma((D,)), dma((8,)), dma((8,)),
        *[dma((D,))] * 4, dma((5,)),
    ]
    return pl.pallas_call(
        kernel,
        out_shape=(jax.ShapeDtypeStruct((N, K), BF16), jax.ShapeDtypeStruct((K, K), F32), jax.ShapeDtypeStruct((K, K), F32)),
        in_specs=[any_spec] * 9 + [pl.BlockSpec(memory_space=pltpu.SMEM)],
        out_specs=(any_spec, any_spec, any_spec),
        scratch_shapes=scratch,
        compiler_params=pltpu.CompilerParams(
            collective_id=0, has_side_effects=True, vmem_limit_bytes=60 * 1024 * 1024),
    )(*args)


def solution(mesh):
    in_specs = (
        P(GRP_LEAF, None), P(GRP_LEAF, None), P(GRP_LEAF, None), P(GRP_LEAF, None, None), P(GRP_LEAF, None, None),
        P(GRP_LEAF, None, None), P(None, GRP_LEAF, None, None), P(None, "grp", None, None), P(), P(),
    )
    return jax.shard_map(
        body, mesh=mesh, in_specs=in_specs, out_specs=(P(GRP_LEAF, None), P(), P()), check_vma=False)
```

time: 178 us -> 56.6 us (0.32)
  blocking collectives: 69.6 us -> 0 us
  Pallas kernels: 0 us -> 49.7 us
  starting transfers between devices: 31.4 us -> 0 us
  matrix products: 27.6 us -> 0 us
  waiting for transfers between devices: 18.6 us -> 0 us
  local copies, waits for them, and re-layouts: 23.1 us -> 5.4 us
  other arithmetic: 5.4 us -> 0 us
    all_to_all x4 -> x0, blocking collectives: 69.6 us -> none  [the longest x2 32.2 us: copy_for_each(): return lax.all_to_all(copies, axis, split_axis=0, concat_axis=0, tiled=True)]
    pallas_call x0 -> x1, Pallas kernels: none -> 49.7 us  [body(): pl.pallas_call(kernel, out_shape=(jax.ShapeDtypeStruct((N, K), BF16), jax...]
    ppermute x15 -> x0, starting transfers between devices: 31.4 us -> none  [from_partner(): return lax.ppermute(block, axis, route)]
    dot_general x20 -> x0, matrix products: 27.6 us -> none  [the longest x8 8.23 us: body(): passed = jnp.dot(operators[1], coarse, preferred_element_type=jnp.float32)]
    ppermute x15 -> x0, waiting for transfers between devices: 18.6 us -> none  [from_partner(): return lax.ppermute(block, axis, route)]
    scatter x1 -> x0, local copies, waits for them, and re-layouts: 8.56 us -> none  [body(): restored = jnp.zeros(local.shape, jnp.float32).at[ordering].set(local)]
    gather x1 -> x0, local copies, waits for them, and re-layouts: 5.81 us -> none  [body(): ordered = jnp.take(direction, ordering, axis=0)]
    unnamed x11 -> x3, local copies, waits for them, and re-layouts: 1.53 us -> 5.4 us
  transfers between devices with their start and end apart: 15 -> 0, of which waited for: 8 -> 0; matrix products, arithmetic and copies ran while one was open for 9% -> 0% of each run, Pallas kernels for 0% -> 0%
where the time goes in v1:
time: 56.6 us; the launch traced here: 56.4 us
  Pallas kernels  49.7 us (88%)
  local copies, waits for them, and re-layouts  5.4 us (10%)
  between operations  1.29 us (2%)
    pallas_call x1, Pallas kernels, body(): pl.pallas_call(kernel, out_shape=(jax.ShapeDtypeStruct((N, K), BF16), jax...  49.7 us
    unnamed x3, local copies, waits for them, and re-layouts  5.4 us

profile of v1, /device:TPU:1, one launch (start us, length us, event | category | flops | bytes accessed | tf_op | source)
XLA Modules:
  0.0 56.4 jit_solution(4515248564107820806)
XLA Ops:
  1.3 49.7 %shard_map.121 = (bf16[1536,256]{1,0:T(8,128)(2,1)}, f32[256,256]{1,0:T(8,128)}, f32[256,256]{1,0:T(8,128)}) custom-call(bf16[1536,256]{1,0:T(8,128)(2,1)} %x_h.1, bf16[1536,256]{1,0:T(8,128)(2,1)} %res_h.1, s32[1,1536]{1,0:T(1,128)} %ord_h.1, bf16[1,1536,1536]{2,1,0:T(8,128)(2,1)} %diag_h.1, bf16[1,1536,128]{2,1,0:T(8,128)(2,1)} %up_h.1, ...), custom_call_target="tpu_custom_call" | custom-call | tf_op jit(solution)/shard_map/pallas_call | solution.py:300
  51.0 2.1 %copy.17 = bf16[1536,256]{1,0:T(8,128)(2,1)} copy(bf16[1536,256]{1,0:T(8,128)(2,1)} %get-tuple-element.6) | data formatting | bytes 1572864
  53.0 1.7 %copy.18 = f32[256,256]{1,0:T(8,128)} copy(f32[256,256]{1,0:T(8,128)} %get-tuple-element.7) | data formatting | bytes 524288
  54.7 1.7 %copy.19 = f32[256,256]{1,0:T(8,128)} copy(f32[256,256]{1,0:T(8,128)} %get-tuple-element.8) | data formatting | bytes 524288

commit v2 on v1

v2 whole, which is shorter than its diff:
```python
import jax
import jax.numpy as jnp
from jax import lax
from jax.experimental import pallas as pl
from jax.experimental.pallas import tpu as pltpu
from jax.sharding import PartitionSpec as P

F32 = jnp.float32
BF16 = jnp.bfloat16
GRP_LEAF = ("grp", "leaf")
N = 1536
R = 128
K = 256
D = 16
C = K // D


def mm(a, b):
    return lax.dot_general(a, b, (((1,), (0,)), ((), ())), preferred_element_type=F32)


def mmt(a, b):
    return lax.dot_general(a, b, (((1,), (1,)), ((), ())), preferred_element_type=F32)


def kernel(
    x_h, res_h, ord_h, diag_h, up_h, dn_h, lop_h, iop_h, top_h, ridge_s,
    img_v, out_v,
    x_v, res_v, ord_v, diag_v, up_v, dn_v, lop_v, iop_v, w_v, rp_v, bp_v,
    p_v, pt_v, og_v, xt_v, loc_v, im_v,
    s0_v, sib_v, l1_v, a_r, root_v, b_r, t_v, q_v, vr_v, xv_v, c_v, c_r,
    pre_v, gs_v, gs_r, h_v, h_r, z_v, z_r, f_v, f_r, o_r,
    load_sem, pair_s, pair_r, a_ss, a_rs, b_ss, b_rs, c_ss, c_rs,
    h_ss, h_rs, z_ss, z_rs, f_ss, f_rs, o_ss, o_rs,
):
    me = lax.axis_index("leaf")
    g = lax.axis_index("grp")
    core = lax.rem(me, 2)
    z = me // 2
    sibling = me + 1 - 2 * core

    leaf_peers = [lax.rem(me + r, D) for r in sorted(range(1, D), key=lambda r: -min(r, D - r))]
    z_peers = [lax.rem(me + 2 * r, D) for r in sorted(range(1, D // 2), key=lambda r: -min(r, D // 2 - r))]
    steps = sorted(((dy, dx) for dy in range(4) for dx in range(4) if dy or dx),
                   key=lambda s: -(min(s[0], 4 - s[0]) + min(s[1], 4 - s[1])))
    gy, gx = g // 4, lax.rem(g, 4)
    grp_peers = [lax.rem(gy + dy, 4) * 4 + lax.rem(gx + dx, 4) for dy, dx in steps]

    def sib_of(a):
        return a + 1 - 2 * lax.rem(a, 2)

    def remote(axis, src, dst, ss, rs, j):
        return pltpu.make_async_remote_copy(
            src_ref=src, dst_ref=dst, send_sem=ss, recv_sem=rs,
            device_id={axis: j}, device_id_type=pl.DeviceIdType.MESH)

    a4, a5, a6, a7 = g, g // 2, g // 4, g // 8
    pairs = [
        (ord_h, ord_v), (up_h.at[0], up_v), (lop_h.at[:, 0], lop_v), (x_h, x_v),
        (iop_h, iop_v), (top_h.at[0, 0:28], w_v),
        (top_h.at[1, a4], rp_v.at[0]), (top_h.at[1, 16 + a5], rp_v.at[1]), (top_h.at[1, 24 + a6], rp_v.at[2]),
        (top_h.at[2, a4], bp_v.at[0]), (top_h.at[2, 16 + a5], bp_v.at[1]), (top_h.at[2, 24 + a6], bp_v.at[2]),
        (top_h.at[2, 28 + a7], bp_v.at[3]),
        (dn_h.at[0], dn_v), (diag_h.at[0], diag_v), (res_h, res_v),
    ]
    loads = [pltpu.make_async_copy(src, dst, load_sem.at[i]) for i, (src, dst) in enumerate(pairs)]
    l_ord, l_up, l_lop, l_x, l_iop = loads[:5]
    l_top = loads[5:13]
    l_dn, l_diag, l_res = loads[13:]
    for copy in loads[:4]:
        copy.start()

    barrier = pltpu.get_barrier_semaphore()
    for j in leaf_peers:
        pl.semaphore_signal(barrier, inc=1, device_id={"leaf": j}, device_id_type=pl.DeviceIdType.MESH)
    for j in grp_peers:
        pl.semaphore_signal(barrier, inc=1, device_id={"grp": j}, device_id_type=pl.DeviceIdType.MESH)

    l_ord.wait()
    order = ord_v[...]
    column = jnp.broadcast_to(order.astype(F32), (R, N)).T.astype(jnp.int32)
    lane = lax.broadcasted_iota(jnp.int32, (N, R), 1)
    low = jnp.where((column & (R - 1)) == lane, 1.0, 0.0).astype(BF16)
    high = (column >> 7).astype(BF16)
    for j in range(N // R):
        p_v[:, j * R:(j + 1) * R] = jnp.where(high == jnp.asarray(j, BF16), low, jnp.zeros_like(low))

    l_up.wait()
    l_lop.wait()
    up_t = up_v[...].T
    lift_t = lax.dot_general(lop_v[0], up_t, (((0,), (0,)), ((), ())), preferred_element_type=F32).astype(BF16)
    both_t = jnp.concatenate([up_t, lift_t], axis=0)

    l_x.wait()
    for copy in loads[4:]:
        copy.start()
    for t in range(3):
        rows = pl.ds(t * 512, 512)
        og_v[rows, :] = mm(p_v[rows, :], x_v[...]).astype(BF16)
    both = mm(both_t, og_v[...]).T
    s0_v[...] = both[:, :R].astype(BF16)
    l1_v[...] = both[:, R:].astype(BF16).reshape(D, C, R)

    pl.semaphore_wait(barrier, 2 * (D - 1))

    sends = []

    def send(*args):
        copy = remote(*args)
        copy.start()
        sends.append(copy)
        return copy

    for i, j in enumerate(leaf_peers):
        send("leaf", l1_v.at[j], a_r.at[me], a_ss.at[i], a_rs.at[me], j)
    pair = send("leaf", s0_v, sib_v, pair_s.at[0], pair_r.at[0], sibling)
    a_r[me] = l1_v[me]

    l_iop.wait()
    up2 = [mm(iop_v[0, 8 + 2 * m:10 + 2 * m].reshape(2 * R, R), iop_v[0, 12 + m]).astype(BF16) for m in range(2)]
    up1 = [mm(iop_v[0, 2 * m:2 * m + 2].reshape(2 * R, R), up2[m // 2][(m % 2) * R:(m % 2 + 1) * R]).astype(BF16)
           for m in range(4)]
    q2 = [mm(iop_v[1, 8 + m], iop_v[1, 12 + m // 2]).astype(BF16) for m in range(4)]
    for m in range(8):
        q_v[m] = mm(iop_v[1, m], q2[m // 2]).astype(BF16)
    for copy in l_top:
        copy.wait()
    y5 = rp_v[0]
    y6 = mm(y5, rp_v[1]).astype(BF16)
    y7 = mm(y6, rp_v[2]).astype(BF16)
    x5 = mm(y5, bp_v[1]).astype(BF16)
    x6 = mm(y6, bp_v[2]).astype(BF16)
    x7 = mm(y7, bp_v[3]).astype(BF16)

    def lifts(base, node, count):
        return w_v[pl.ds(base + node, count)].reshape(count * R, R)

    t_v[g] = jnp.zeros((R, R), BF16)
    n4, n5, n6, n7 = sib_of(a4), sib_of(a5), sib_of(a6), sib_of(a7)
    t_v[n4] = bp_v[0].T
    t_v[pl.ds(2 * n5, 2)] = mmt(lifts(0, 2 * n5, 2), x5).astype(BF16).reshape(2, R, R)
    w = mmt(lifts(16, 2 * n6, 2), x6).astype(BF16)
    for b in range(2):
        t_v[pl.ds(4 * n6 + 2 * b, 2)] = mm(lifts(0, 4 * n6 + 2 * b, 2), w[b * R:(b + 1) * R]).astype(BF16).reshape(2, R, R)
    w = mmt(lifts(24, 2 * n7, 2), x7).astype(BF16)
    for b in range(2):
        u = mm(lifts(16, 4 * n7 + 2 * b, 2), w[b * R:(b + 1) * R]).astype(BF16)
        for d in range(2):
            first = 8 * n7 + 4 * b + 2 * d
            t_v[pl.ds(first, 2)] = mm(lifts(0, first, 2), u[d * R:(d + 1) * R]).astype(BF16).reshape(2, R, R)

    row_low = jnp.broadcast_to(order & (R - 1), (R, N))
    row_high = jnp.broadcast_to(order >> 7, (R, N)).astype(F32).astype(BF16)
    row_one = jnp.where(row_low == lax.broadcasted_iota(jnp.int32, (R, N), 0), 1.0, 0.0).astype(BF16)
    for j in range(N // R):
        pt_v[j * R:(j + 1) * R, :] = jnp.where(row_high == jnp.asarray(j, BF16), row_one, jnp.zeros_like(row_one))
    l_dn.wait()
    vr_v[...] = mm(dn_v[...], lop_v[1]).astype(BF16)
    xt_v[:K, :] = og_v[...].T
    l_diag.wait()
    ridge = ridge_s[0]
    for t in range(3):
        rows = pl.ds(t * 512, 512)
        loc_v[rows, :] = mm(diag_v[rows, :], og_v[...]) + ridge * og_v[rows, :].astype(F32)

    for i, j in enumerate(leaf_peers):
        remote("leaf", l1_v.at[j], a_r.at[j], a_ss.at[i], a_rs.at[j], j).wait_recv()
    s1 = [(a_r[2 * m].astype(F32) + a_r[2 * m + 1].astype(F32)).astype(BF16) for m in range(8)]
    s1p = [jnp.concatenate(s1[2 * m:2 * m + 2], axis=1) for m in range(4)]
    root = mm(s1p[0], up1[0])
    for m in range(1, 4):
        root = root + mm(s1p[m], up1[m])
    root_v[...] = root.astype(BF16)

    for i, j in enumerate(grp_peers):
        send("grp", root_v, b_r.at[g], b_ss.at[i], b_rs.at[g], j)
    b_r[g] = root_v[...]

    s2 = [mm(s1p[m], iop_v[0, 2 * m:2 * m + 2].reshape(2 * R, R)).astype(BF16) for m in range(4)]
    s2p = [jnp.concatenate(s2[2 * m:2 * m + 2], axis=1) for m in range(2)]
    s3 = [mm(s2p[m], iop_v[0, 8 + 2 * m:10 + 2 * m].reshape(2 * R, R)).astype(BF16) for m in range(2)]
    c3 = [mmt(s3[1 - m], iop_v[2, 12 + m]).astype(BF16) for m in range(2)]
    c2 = [(mmt(s2[m ^ 1], iop_v[2, 8 + m]) + mmt(c3[m // 2], iop_v[1, 8 + m])).astype(BF16) for m in range(4)]
    c1 = [mmt(s1[m ^ 1], iop_v[2, m]) + mmt(c2[m // 2], iop_v[1, m]) for m in range(8)]
    pair.wait_recv()
    near = mmt(sib_v[...], lop_v[2]).astype(BF16)
    loc_v[...] = loc_v[...] + mmt(dn_v[...], near)
    l_res.wait()
    for t in range(3):
        rows = pl.ds(t * 512, 512)
        xt_v[K:, rows] = mm(p_v[rows, :], res_v[...]).astype(BF16).T

    for i, j in enumerate(grp_peers):
        remote("grp", root_v, b_r.at[j], b_ss.at[i], b_rs.at[j], j).wait_recv()
    c4 = jnp.zeros((C, R), F32)
    for m in range(D // 2):
        c4 = c4 + mm(jnp.concatenate([b_r[2 * m], b_r[2 * m + 1]], axis=1), t_v[2 * m:2 * m + 2].reshape(2 * R, R))
    c4 = c4.astype(BF16)
    for m in range(8):
        c_v[m] = (c1[m] + mmt(c4, q_v[m])).astype(BF16)

    for i, j in enumerate(leaf_peers):
        send("leaf", c_v.at[j // 2], c_r.at[me], c_ss.at[i], c_rs.at[me], j)
    c_r[me] = c_v[z]

    im_v[...] = loc_v[...].astype(BF16)
    for t in range(2):
        pre_v[t] = mm(xt_v[t * K:(t + 1) * K, :], im_v[...])
    xv_v[...] = mm(xt_v[...], vr_v[...]).astype(BF16).reshape(2, K, R)

    for i, j in enumerate(leaf_peers):
        remote("leaf", c_v.at[j // 2], c_r.at[j], c_ss.at[i], c_rs.at[j], j).wait_recv()

    coarse = c_r[...].reshape(K, R)
    gs_v[...] = (pre_v[1 - core] + mmt(xv_v[1 - core], coarse)).astype(BF16)
    swap = send("leaf", gs_v, gs_r, pair_s.at[1], pair_r.at[1], sibling)
    own = pre_v[core] + mmt(xv_v[core], coarse)
    im_v[...] = (loc_v[...] + mmt(vr_v[...], coarse)).astype(BF16)
    swap.wait_recv()
    h_v[...] = (own + gs_r[...].astype(F32)).astype(BF16).reshape(D, C, K)
    for i, j in enumerate(grp_peers):
        send("grp", h_v.at[j], h_r.at[g], h_ss.at[i], h_rs.at[g], j)
    h_r[g] = h_v[g]

    for t in range(3):
        rows = pl.ds(t * 512, 512)
        img_v[rows, :] = mm(pt_v[rows, :], im_v[...]).astype(BF16)

    for i, j in enumerate(grp_peers):
        remote("grp", h_v.at[j], h_r.at[j], h_ss.at[i], h_rs.at[j], j).wait_recv()
    total = h_r[0].astype(F32)
    for j in range(1, D):
        total = total + h_r[j].astype(F32)
    z_v[...] = total.astype(BF16)
    for i, j in enumerate(z_peers):
        send("leaf", z_v, z_r.at[z], z_ss.at[i], z_rs.at[z], j)
    z_r[z] = z_v[...]
    for i, j in enumerate(z_peers):
        remote("leaf", z_v, z_r.at[j // 2], z_ss.at[i], z_rs.at[j // 2], j).wait_recv()
    total = z_r[0].astype(F32)
    for j in range(1, D // 2):
        total = total + z_r[j].astype(F32)
    f_v[...] = total.astype(BF16)
    for i, j in enumerate(grp_peers):
        send("grp", f_v, f_r.at[g], f_ss.at[i], f_rs.at[g], j)
    f_r[g] = f_v[...]
    send("leaf", f_v, o_r.at[g], o_ss.at[g], o_rs.at[g], sibling)
    for i, j in reversed(list(enumerate(grp_peers))):
        remote("grp", f_v, f_r.at[j], f_ss.at[i], f_rs.at[j], j).wait_recv()
        send("leaf", f_r.at[j], o_r.at[j], o_ss.at[j], o_rs.at[j], sibling)
    scale = 1.0 / (N * D * D)
    out_v[core] = f_r[...].reshape(K, K).astype(F32) * scale
    for j in range(D):
        remote("leaf", f_r.at[j], o_r.at[j], o_ss.at[j], o_rs.at[j], sibling).wait_recv()
    out_v[1 - core] = o_r[...].reshape(K, K).astype(F32) * scale
    for copy in sends:
        copy.wait_send()


def finish(image, grams, img_h, cur_h, cor_h, sem):
    copies = [
        pltpu.make_async_copy(src, dst, sem.at[i])
        for i, (src, dst) in enumerate(((image, img_h), (grams.at[0], cur_h), (grams.at[1], cor_h)))
    ]
    for copy in copies:
        copy.start()
    for copy in copies:
        copy.wait()


def body(*args):
    any_spec = pl.BlockSpec(memory_space=pl.ANY)
    vmem_spec = pl.BlockSpec(memory_space=pltpu.VMEM)
    dma = pltpu.SemaphoreType.DMA
    v = pltpu.VMEM
    scratch = [
        v((N, K), BF16), v((N, K), BF16), v((1, N), jnp.int32), v((N, N), BF16), v((N, R), BF16), v((N, R), BF16),
        v((3, R, R), BF16), v((3, 14, R, R), BF16), v((28, R, R), BF16), v((3, R, R), BF16), v((4, R, R), BF16),
        v((N, N), BF16), v((N, N), BF16), v((N, K), BF16), v((2 * K, N), BF16), v((N, K), F32), v((N, K), BF16),
        v((K, R), BF16), v((K, R), BF16), v((D, C, R), BF16), v((D, C, R), BF16), v((C, R), BF16), v((D, C, R), BF16),
        v((D, R, R), BF16), v((8, R, R), BF16), v((N, R), BF16), v((2, K, R), BF16), v((8, C, R), BF16), v((D, C, R), BF16),
        v((2, K, K), F32), v((K, K), BF16), v((K, K), BF16), v((D, C, K), BF16), v((D, C, K), BF16), v((C, K), BF16),
        v((8, C, K), BF16), v((C, K), BF16), v((D, C, K), BF16), v((D, C, K), BF16),
        dma((16,)), dma((2,)), dma((2,)), *[dma((D,))] * 6, dma((D,)), dma((D,)), dma((8,)), dma((8,)), *[dma((D,))] * 4,
    ]
    args = [pltpu.with_memory_space_constraint(a, pltpu.HBM) for a in args[:-1]] + [args[-1]]
    image, grams = pl.pallas_call(
        kernel,
        out_shape=(jax.ShapeDtypeStruct((N, K), BF16), jax.ShapeDtypeStruct((2, K, K), F32)),
        in_specs=[any_spec] * 9 + [pl.BlockSpec(memory_space=pltpu.SMEM)],
        out_specs=(vmem_spec, vmem_spec),
        scratch_shapes=scratch,
        compiler_params=pltpu.CompilerParams(
            collective_id=0, has_side_effects=True, vmem_limit_bytes=48 * 1024 * 1024),
    )(*args)
    return pl.pallas_call(
        finish,
        out_shape=(jax.ShapeDtypeStruct((N, K), BF16), jax.ShapeDtypeStruct((K, K), F32), jax.ShapeDtypeStruct((K, K), F32)),
        in_specs=[any_spec, any_spec],
        out_specs=(any_spec, any_spec, any_spec),
        scratch_shapes=[dma((3,))],
        compiler_params=pltpu.CompilerParams(vmem_limit_bytes=1024 * 1024),
    )(image, grams)


def solution(mesh):
    in_specs = (
        P(GRP_LEAF, None), P(GRP_LEAF, None), P(GRP_LEAF, None), P(GRP_LEAF, None, None), P(GRP_LEAF, None, None),
        P(GRP_LEAF, None, None), P(None, GRP_LEAF, None, None), P(None, "grp", None, None), P(), P(),
    )
    return jax.shard_map(
        body, mesh=mesh, in_specs=in_specs, out_specs=(P(GRP_LEAF, None), P(), P()), check_vma=False)
```

time: 56.6 us -> 49 us (0.87)
  local copies, waits for them, and re-layouts: 5.4 us -> 0 us
  Pallas kernels: 49.7 us -> 47.6 us
    unnamed x3 -> x0, local copies, waits for them, and re-layouts: 5.4 us -> none
    pallas_call x1, Pallas kernels: 49.7 us -> 46.5 us  [body(): pl.pallas_call(kernel, out_shape=(jax.ShapeDtypeStruct((N, K), BF16), jax...]
    pallas_call x0 -> x1, Pallas kernels: none -> 1.08 us  [body(): pl.pallas_call(finish, out_shape=(jax.ShapeDtypeStruct((N, K), BF16), jax...]
where the time goes in v2:
time: 49 us; the launch traced here: 48.9 us
  Pallas kernels  47.6 us (97%)
  between operations  1.29 us (3%)
    pallas_call x1, Pallas kernels, body(): pl.pallas_call(kernel, out_shape=(jax.ShapeDtypeStruct((N, K), BF16), jax...  46.5 us
    pallas_call x1, Pallas kernels, body(): pl.pallas_call(finish, out_shape=(jax.ShapeDtypeStruct((N, K), BF16), jax...  1.08 us

profile of v2, /device:TPU:1, one launch (start us, length us, event | category | flops | bytes accessed | tf_op | source)
XLA Modules:
  0.0 48.9 jit_solution(6036042771345343722)
XLA Ops:
  1.3 46.5 %shard_map.121 = (bf16[1536,256]{1,0:T(8,128)(2,1)S(1)}, f32[2,256,256]{2,1,0:T(8,128)S(1)}) custom-call(bf16[1536,256]{1,0:T(8,128)(2,1)} %x_h.1, bf16[1536,256]{1,0:T(8,128)(2,1)} %res_h.1, s32[1,1536]{1,0:T(1,128)} %ord_h.1, bf16[1,1536,1536]{2,1,0:T(8,128)(2,1)} %diag_h.1, bf16[1,1536,128]{2,1,0:T(8,128)(2,1)} %up_h.1, bf16[1,1536,128]{2,1,0:T(8,128)(2,1)} %dn_h.1, ...), custom_call_target="tpu_custom_call" | custom-call | tf_op jit(solution)/shard_map/pallas_call | solution.py:287
  47.8 1.1 %shard_map.122 = (bf16[1536,256]{1,0:T(8,128)(2,1)}, f32[256,256]{1,0:T(8,128)}, f32[256,256]{1,0:T(8,128)}) custom-call(bf16[1536,256]{1,0:T(8,128)(2,1)S(1)} %get-tuple-element.5.image, f32[2,256,256]{2,1,0:T(8,128)S(1)} %get-tuple-element.6.grams), custom_call_target="tpu_custom_call" | custom-call | tf_op jit(solution)/shard_map/pallas_call | solution.py:296

commit v3 on v2

v3 whole, which is shorter than its diff:
```python
import jax
import jax.numpy as jnp
from jax import lax
from jax.experimental import pallas as pl
from jax.experimental.pallas import tpu as pltpu
from jax.sharding import PartitionSpec as P

F32 = jnp.float32
BF16 = jnp.bfloat16
GRP_LEAF = ("grp", "leaf")
N = 1536
R = 128
K = 256
D = 16
C = K // D


def mm(a, b):
    return lax.dot_general(a, b, (((1,), (0,)), ((), ())), preferred_element_type=F32)


def mmt(a, b):
    return lax.dot_general(a, b, (((1,), (1,)), ((), ())), preferred_element_type=F32)


def kernel(
    x_h, res_h, ord_h, diag_h, up_h, dn_h, lop_h, iop_h, top_h, ridge_s,
    img_v, out_v,
    x_v, res_v, ord_v, diag_v, up_v, dn_v, lop_v, iop_v, w_v, path_v,
    p_v, pt_v, og_v, xt_v, loc_v, im_v,
    s0_v, sib_v, l1_v, a_r, root_v, b_r, t_v, u_v, q_v, vr_v, xv_v, c_v, c_r,
    pre_v, gs_v, gs_r, h_v, h_r, z_v, z_r, f_v, f_r, o_r,
    load_sem, send_sem, recv_sem,
):
    me = lax.axis_index("leaf")
    g = lax.axis_index("grp")
    core = lax.rem(me, 2)
    z = me // 2
    sibling = me + 1 - 2 * core

    leaf_peers = [lax.rem(me + r, D) for r in sorted(range(1, D), key=lambda r: -min(r, D - r))]
    z_peers = [lax.rem(me + 2 * r, D) for r in sorted(range(1, D // 2), key=lambda r: -min(r, D // 2 - r))]
    steps = sorted(((dy, dx) for dy in range(4) for dx in range(4) if dy or dx),
                   key=lambda s: -(min(s[0], 4 - s[0]) + min(s[1], 4 - s[1])))
    gy, gx = g // 4, lax.rem(g, 4)
    grp_peers = [lax.rem(gy + dy, 4) * 4 + lax.rem(gx + dx, 4) for dy, dx in steps]

    def sib_of(a):
        return a + 1 - 2 * lax.rem(a, 2)

    def remote(phase, axis, src, dst, j):
        return pltpu.make_async_remote_copy(
            src_ref=src, dst_ref=dst, send_sem=send_sem.at[phase], recv_sem=recv_sem.at[phase],
            device_id={axis: j}, device_id_type=pl.DeviceIdType.MESH)

    def arrived(phase, ref):
        remote(phase, "leaf", ref, ref, sibling).wait_recv()

    def left(phase, ref):
        remote(phase, "leaf", ref, ref, sibling).wait_send()

    a4, a5, a6, a7 = g, g // 2, g // 4, g // 8
    def start_all(copies):
        for copy in copies:
            copy.start()

    def load(slot, src, dst):
        return pltpu.make_async_copy(src, dst, load_sem.at[slot])

    l_ord = load(0, ord_h, ord_v)
    l_up = load(1, up_h.at[0], up_v)
    l_lop = load(2, lop_h.at[:, 0], lop_v)
    l_x = load(3, x_h, x_v)
    start_all([l_ord, l_up, l_lop, l_x])
    l_iop = load(4, iop_h, iop_v)
    l_lift = load(5, top_h.at[0, 0:28], w_v)
    path = [(1, a4), (1, 16 + a5), (1, 24 + a6), (2, a4), (2, 16 + a5), (2, 24 + a6), (2, 28 + a7)]
    l_path = [load(6, top_h.at[kind, node], path_v.at[i]) for i, (kind, node) in enumerate(path)]
    l_dn = load(7, dn_h.at[0], dn_v)
    l_diag = load(8, diag_h.at[0], diag_v)
    l_res = load(9, res_h, res_v)

    barrier = pltpu.get_barrier_semaphore()
    for j in leaf_peers:
        pl.semaphore_signal(barrier, inc=1, device_id={"leaf": j}, device_id_type=pl.DeviceIdType.MESH)
    for j in grp_peers:
        pl.semaphore_signal(barrier, inc=1, device_id={"grp": j}, device_id_type=pl.DeviceIdType.MESH)

    l_ord.wait()
    order = ord_v[...]
    column = jnp.broadcast_to(order.astype(F32), (R, N)).T.astype(jnp.int32)
    lane = lax.broadcasted_iota(jnp.int32, (N, R), 1)
    low = jnp.where((column & (R - 1)) == lane, 1.0, 0.0).astype(BF16)
    high = (column >> 7).astype(BF16)
    for j in range(N // R):
        p_v[:, j * R:(j + 1) * R] = jnp.where(high == jnp.asarray(j, BF16), low, jnp.zeros_like(low))

    l_up.wait()
    l_lop.wait()
    up_t = up_v[...].T
    lift_t = lax.dot_general(lop_v[0], up_t, (((0,), (0,)), ((), ())), preferred_element_type=F32).astype(BF16)
    both_t = jnp.concatenate([up_t, lift_t], axis=0)

    both_t = mm(both_t, p_v[...]).astype(BF16)
    l_x.wait()
    start_all([l_iop, l_lift, *l_path, l_dn, l_diag, l_res])
    both = mm(both_t, x_v[...]).T
    s0_v[...] = both[:, :R].astype(BF16)
    l1_v[...] = both[:, R:].astype(BF16).reshape(D, C, R)

    pl.semaphore_wait(barrier, 2 * (D - 1))

    for j in leaf_peers:
        remote(0, "leaf", l1_v.at[j], a_r.at[me], j).start()
    remote(1, "leaf", s0_v, sib_v, sibling).start()
    a_r[me] = l1_v[me]

    for t in range(3):
        rows = pl.ds(t * 512, 512)
        og_v[rows, :] = mm(p_v[rows, :], x_v[...]).astype(BF16)
    l_iop.wait()
    up2 = [mm(iop_v[0, 8 + 2 * m:10 + 2 * m].reshape(2 * R, R), iop_v[0, 12 + m]).astype(BF16) for m in range(2)]
    for m in range(4):
        u_v[2 * R * m:2 * R * (m + 1), :] = mm(
            iop_v[0, 2 * m:2 * m + 2].reshape(2 * R, R), up2[m // 2][(m % 2) * R:(m % 2 + 1) * R]).astype(BF16)
    q2 = [mm(iop_v[1, 8 + m], iop_v[1, 12 + m // 2]).astype(BF16) for m in range(4)]
    for m in range(8):
        q_v[m * R:(m + 1) * R, :] = mm(iop_v[1, m], q2[m // 2]).astype(BF16)
    l_lift.wait()
    load(6, top_h.at[1, 0:7], path_v).wait()
    y5 = path_v[0]
    y6 = mm(y5, path_v[1]).astype(BF16)
    y7 = mm(y6, path_v[2]).astype(BF16)
    x5 = mm(y5, path_v[4]).astype(BF16)
    x6 = mm(y6, path_v[5]).astype(BF16)
    x7 = mm(y7, path_v[6]).astype(BF16)

    def lifts(base, node, count):
        return w_v[pl.ds(base + node, count)].reshape(count * R, R)

    t_v[g] = jnp.zeros((R, R), BF16)
    n4, n5, n6, n7 = sib_of(a4), sib_of(a5), sib_of(a6), sib_of(a7)
    t_v[n4] = path_v[3].T
    t_v[pl.ds(2 * n5, 2)] = mmt(lifts(0, 2 * n5, 2), x5).astype(BF16).reshape(2, R, R)
    w = mmt(lifts(16, 2 * n6, 2), x6).astype(BF16)
    for b in range(2):
        t_v[pl.ds(4 * n6 + 2 * b, 2)] = mm(lifts(0, 4 * n6 + 2 * b, 2), w[b * R:(b + 1) * R]).astype(BF16).reshape(2, R, R)
    w = mmt(lifts(24, 2 * n7, 2), x7).astype(BF16)
    for b in range(2):
        u = mm(lifts(16, 4 * n7 + 2 * b, 2), w[b * R:(b + 1) * R]).astype(BF16)
        for d in range(2):
            first = 8 * n7 + 4 * b + 2 * d
            t_v[pl.ds(first, 2)] = mm(lifts(0, first, 2), u[d * R:(d + 1) * R]).astype(BF16).reshape(2, R, R)

    row_low = jnp.broadcast_to(order & (R - 1), (R, N))
    row_high = jnp.broadcast_to(order >> 7, (R, N)).astype(F32).astype(BF16)
    row_one = jnp.where(row_low == lax.broadcasted_iota(jnp.int32, (R, N), 0), 1.0, 0.0).astype(BF16)
    for j in range(N // R):
        pt_v[j * R:(j + 1) * R, :] = jnp.where(row_high == jnp.asarray(j, BF16), row_one, jnp.zeros_like(row_one))
    l_dn.wait()
    vr_v[...] = mm(dn_v[...], lop_v[1]).astype(BF16)
    xt_v[:K, :] = og_v[...].T
    l_diag.wait()
    ridge = ridge_s[0]
    for t in range(3):
        rows = pl.ds(t * 512, 512)
        loc_v[rows, :] = mm(diag_v[rows, :], og_v[...]) + ridge * og_v[rows, :].astype(F32)

    arrived(0, a_r.at[0:15])
    s1 = [(a_r[2 * m].astype(F32) + a_r[2 * m + 1].astype(F32)).astype(BF16) for m in range(8)]
    s1p = [jnp.concatenate(s1[2 * m:2 * m + 2], axis=1) for m in range(4)]
    root_v[...] = mm(jnp.concatenate(s1, axis=1), u_v[...]).astype(BF16)

    for j in grp_peers:
        remote(2, "grp", root_v, b_r.at[g], j).start()
    b_r[g] = root_v[...]

    s2 = [mm(s1p[m], iop_v[0, 2 * m:2 * m + 2].reshape(2 * R, R)).astype(BF16) for m in range(4)]
    s2p = [jnp.concatenate(s2[2 * m:2 * m + 2], axis=1) for m in range(2)]
    s3 = [mm(s2p[m], iop_v[0, 8 + 2 * m:10 + 2 * m].reshape(2 * R, R)).astype(BF16) for m in range(2)]
    c3 = [mmt(s3[1 - m], iop_v[2, 12 + m]).astype(BF16) for m in range(2)]
    c2 = [(mmt(s2[m ^ 1], iop_v[2, 8 + m]) + mmt(c3[m // 2], iop_v[1, 8 + m])).astype(BF16) for m in range(4)]
    c1 = [mmt(s1[m ^ 1], iop_v[2, m]) + mmt(c2[m // 2], iop_v[1, m]) for m in range(8)]
    arrived(1, sib_v)
    near = mmt(sib_v[...], lop_v[2]).astype(BF16)
    loc_v[...] = loc_v[...] + mmt(dn_v[...], near)
    l_res.wait()
    for t in range(3):
        rows = pl.ds(t * 512, 512)
        xt_v[K:, rows] = mm(p_v[rows, :], res_v[...]).astype(BF16).T

    arrived(2, b_r.at[0:15])
    c4 = mm(jnp.concatenate([b_r[j] for j in range(D)], axis=1), t_v[...].reshape(D * R, R)).astype(BF16)
    down = mmt(c4, q_v[...])
    for m in range(8):
        c_v[m] = (c1[m] + down[:, m * R:(m + 1) * R]).astype(BF16)

    for j in z_peers:
        remote(3, "leaf", c_v.at[j // 2], c_r.at[z, core], j).start()
    c_r[z, core] = c_v[z]

    im_v[...] = loc_v[...].astype(BF16)
    for t in range(2):
        pre_v[t] = mm(xt_v[t * K:(t + 1) * K, :], im_v[...])
    xv_v[...] = mm(xt_v[...], vr_v[...]).astype(BF16).reshape(2, K, R)

    arrived(3, c_v.at[0:7])
    remote(4, "leaf", c_r.at[:, core], c_r.at[:, core], sibling).start()
    arrived(4, c_v)

    coarse = c_r[...].reshape(K, R)
    gs_v[...] = (pre_v[1 - core] + mmt(xv_v[1 - core], coarse)).astype(BF16)
    remote(5, "leaf", gs_v, gs_r, sibling).start()
    own = pre_v[core] + mmt(xv_v[core], coarse)
    im_v[...] = (loc_v[...] + mmt(vr_v[...], coarse)).astype(BF16)
    arrived(5, gs_r)
    h_v[...] = (own + gs_r[...].astype(F32)).astype(BF16).reshape(D, C, K)
    for j in grp_peers:
        remote(6, "grp", h_v.at[j], h_r.at[g], j).start()
    h_r[g] = h_v[g]

    for t in range(3):
        rows = pl.ds(t * 512, 512)
        img_v[rows, :] = mm(pt_v[rows, :], im_v[...]).astype(BF16)

    arrived(6, h_r.at[0:15])
    total = h_r[0].astype(F32)
    for j in range(1, D):
        total = total + h_r[j].astype(F32)
    z_v[...] = total.astype(BF16)
    for j in z_peers:
        remote(7, "leaf", z_v, z_r.at[z], j).start()
    z_r[z] = z_v[...]
    arrived(7, z_r.at[0:7])
    total = z_r[0].astype(F32)
    for j in range(1, D // 2):
        total = total + z_r[j].astype(F32)
    f_v[...] = total.astype(BF16)
    for j in grp_peers:
        remote(8, "grp", f_v, f_r.at[g], j).start()
    f_r[g] = f_v[...]
    arrived(8, f_r.at[0:15])
    remote(9, "leaf", f_r, o_r, sibling).start()
    scale = 1.0 / (N * D * D)
    out_v[core] = f_r[...].reshape(K, K).astype(F32) * scale
    arrived(9, o_r)
    out_v[1 - core] = o_r[...].reshape(K, K).astype(F32) * scale
    for phase, ref in enumerate((
        l1_v.at[0:15], s0_v, b_r.at[0:15], c_v.at[0:7], c_v, gs_v, h_v.at[0:15], z_r.at[0:7], f_r.at[0:15], f_r,
    )):
        left(phase, ref)


def finish(image, grams, img_h, cur_h, cor_h, sem):
    rows = [pl.ds(t * 256, 256) for t in range(N // 256)]
    pairs = [(image.at[r], img_h.at[r]) for r in rows]
    pairs += [(grams.at[i, pl.ds(t * 128, 128)], dst.at[pl.ds(t * 128, 128)]) for i, dst in enumerate((cur_h, cor_h)) for t in range(2)]
    copies = [pltpu.make_async_copy(src, dst, sem.at[i]) for i, (src, dst) in enumerate(pairs)]
    for copy in copies:
        copy.start()
    for copy in copies:
        copy.wait()


def body(*args):
    any_spec = pl.BlockSpec(memory_space=pl.ANY)
    vmem_spec = pl.BlockSpec(memory_space=pltpu.VMEM)
    dma = pltpu.SemaphoreType.DMA
    v = pltpu.VMEM
    scratch = [
        v((N, K), BF16), v((N, K), BF16), v((1, N), jnp.int32), v((N, N), BF16), v((N, R), BF16), v((N, R), BF16),
        v((3, R, R), BF16), v((3, 14, R, R), BF16), v((28, R, R), BF16), v((7, R, R), BF16),
        v((N, N), BF16), v((N, N), BF16), v((N, K), BF16), v((2 * K, N), BF16), v((N, K), F32), v((N, K), BF16),
        v((K, R), BF16), v((K, R), BF16), v((D, C, R), BF16), v((D, C, R), BF16), v((C, R), BF16), v((D, C, R), BF16),
        v((D, R, R), BF16), v((8 * R, R), BF16), v((8 * R, R), BF16), v((N, R), BF16), v((2, K, R), BF16), v((8, C, R), BF16), v((8, 2, C, R), BF16),
        v((2, K, K), F32), v((K, K), BF16), v((K, K), BF16), v((D, C, K), BF16), v((D, C, K), BF16), v((C, K), BF16),
        v((8, C, K), BF16), v((C, K), BF16), v((D, C, K), BF16), v((D, C, K), BF16),
        dma((10,)), dma((10,)), dma((10,)),
    ]
    args = [pltpu.with_memory_space_constraint(a, pltpu.HBM) for a in args[:-1]] + [args[-1]]
    image, grams = pl.pallas_call(
        kernel,
        out_shape=(jax.ShapeDtypeStruct((N, K), BF16), jax.ShapeDtypeStruct((2, K, K), F32)),
        in_specs=[any_spec] * 9 + [pl.BlockSpec(memory_space=pltpu.SMEM)],
        out_specs=(vmem_spec, vmem_spec),
        scratch_shapes=scratch,
        compiler_params=pltpu.CompilerParams(
            collective_id=0, has_side_effects=True, vmem_limit_bytes=48 * 1024 * 1024),
    )(*args)
    return pl.pallas_call(
        finish,
        out_shape=(jax.ShapeDtypeStruct((N, K), BF16), jax.ShapeDtypeStruct((K, K), F32), jax.ShapeDtypeStruct((K, K), F32)),
        in_specs=[any_spec, any_spec],
        out_specs=(any_spec, any_spec, any_spec),
        scratch_shapes=[dma((10,))],
        compiler_params=pltpu.CompilerParams(vmem_limit_bytes=1024 * 1024),
    )(image, grams)


def solution(mesh):
    in_specs = (
        P(GRP_LEAF, None), P(GRP_LEAF, None), P(GRP_LEAF, None), P(GRP_LEAF, None, None), P(GRP_LEAF, None, None),
        P(GRP_LEAF, None, None), P(None, GRP_LEAF, None, None), P(None, "grp", None, None), P(), P(),
    )
    return jax.shard_map(
        body, mesh=mesh, in_specs=in_specs, out_specs=(P(GRP_LEAF, None), P(), P()), check_vma=False)
```

time: 49 us -> 48.7 us (level)
  no operation moved by 1% of the time
where the time goes in v3:
time: 48.7 us; the launch traced here: 48.6 us
  Pallas kernels  47.3 us (97%)
  between operations  1.29 us (3%)
    pallas_call x1, Pallas kernels, body(): pl.pallas_call(kernel, out_shape=(jax.ShapeDtypeStruct((N, K), BF16), jax...  46.1 us
    pallas_call x1, Pallas kernels, body(): pl.pallas_call(finish, out_shape=(jax.ShapeDtypeStruct((N, K), BF16), jax...  1.13 us

profile of v3, /device:TPU:1, one launch (start us, length us, event | category | flops | bytes accessed | tf_op | source)
XLA Modules:
  0.0 48.6 jit_solution(2170710749590479821)
XLA Ops:
  1.3 46.1 %shard_map.121 = (bf16[1536,256]{1,0:T(8,128)(2,1)S(1)}, f32[2,256,256]{2,1,0:T(8,128)S(1)}) custom-call(bf16[1536,256]{1,0:T(8,128)(2,1)} %x_h.1, bf16[1536,256]{1,0:T(8,128)(2,1)} %res_h.1, s32[1,1536]{1,0:T(1,128)} %ord_h.1, bf16[1,1536,1536]{2,1,0:T(8,128)(2,1)} %diag_h.1, bf16[1,1536,128]{2,1,0:T(8,128)(2,1)} %up_h.1, bf16[1,1536,128]{2,1,0:T(8,128)(2,1)} %dn_h.1, ...), custom_call_target="tpu_custom_call" | custom-call | tf_op jit(solution)/shard_map/pallas_call | solution.py:281
  47.4 1.1 %shard_map.122 = (bf16[1536,256]{1,0:T(8,128)(2,1)}, f32[256,256]{1,0:T(8,128)}, f32[256,256]{1,0:T(8,128)}) custom-call(bf16[1536,256]{1,0:T(8,128)(2,1)S(1)} %get-tuple-element.5.image, f32[2,256,256]{2,1,0:T(8,128)S(1)} %get-tuple-element.6.grams), custom_call_target="tpu_custom_call" | custom-call | tf_op jit(solution)/shard_map/pallas_call | solution.py:290

commit v4 on v3

--- a/solution.py
+++ b/solution.py
@@ -159,12 +159,6 @@
         pt_v[j * R:(j + 1) * R, :] = jnp.where(row_high == jnp.asarray(j, BF16), row_one, jnp.zeros_like(row_one))
     l_dn.wait()
     vr_v[...] = mm(dn_v[...], lop_v[1]).astype(BF16)
-    xt_v[:K, :] = og_v[...].T
-    l_diag.wait()
-    ridge = ridge_s[0]
-    for t in range(3):
-        rows = pl.ds(t * 512, 512)
-        loc_v[rows, :] = mm(diag_v[rows, :], og_v[...]) + ridge * og_v[rows, :].astype(F32)
 
     arrived(0, a_r.at[0:15])
     s1 = [(a_r[2 * m].astype(F32) + a_r[2 * m + 1].astype(F32)).astype(BF16) for m in range(8)]
@@ -181,13 +175,14 @@
     c3 = [mmt(s3[1 - m], iop_v[2, 12 + m]).astype(BF16) for m in range(2)]
     c2 = [(mmt(s2[m ^ 1], iop_v[2, 8 + m]) + mmt(c3[m // 2], iop_v[1, 8 + m])).astype(BF16) for m in range(4)]
     c1 = [mmt(s1[m ^ 1], iop_v[2, m]) + mmt(c2[m // 2], iop_v[1, m]) for m in range(8)]
+    l_diag.wait()
+    ridge = ridge_s[0]
+    for t in range(3):
+        rows = pl.ds(t * 512, 512)
+        loc_v[rows, :] = mm(diag_v[rows, :], og_v[...]) + ridge * og_v[rows, :].astype(F32)
     arrived(1, sib_v)
     near = mmt(sib_v[...], lop_v[2]).astype(BF16)
     loc_v[...] = loc_v[...] + mmt(dn_v[...], near)
-    l_res.wait()
-    for t in range(3):
-        rows = pl.ds(t * 512, 512)
-        xt_v[K:, rows] = mm(p_v[rows, :], res_v[...]).astype(BF16).T
 
     arrived(2, b_r.at[0:15])
     c4 = mm(jnp.concatenate([b_r[j] for j in range(D)], axis=1), t_v[...].reshape(D * R, R)).astype(BF16)
@@ -199,6 +194,11 @@
         remote(3, "leaf", c_v.at[j // 2], c_r.at[z, core], j).start()
     c_r[z, core] = c_v[z]
 
+    xt_v[:K, :] = og_v[...].T
+    l_res.wait()
+    for t in range(3):
+        rows = pl.ds(t * 512, 512)
+        xt_v[K:, rows] = mm(p_v[rows, :], res_v[...]).astype(BF16).T
     im_v[...] = loc_v[...].astype(BF16)
     for t in range(2):
         pre_v[t] = mm(xt_v[t * K:(t + 1) * K, :], im_v[...])

time: 48.7 us -> 47.7 us (0.979)
  Pallas kernels: 47.3 us -> 46.3 us
    pallas_call x1, Pallas kernels: 46.1 us -> 45.1 us  [body(): pl.pallas_call(kernel, out_shape=(jax.ShapeDtypeStruct((N, K), BF16), jax...]
where the time goes in v4:
time: 47.7 us; the launch traced here: 47.6 us
  Pallas kernels  46.3 us (97%)
  between operations  1.29 us (3%)
    pallas_call x1, Pallas kernels, body(): pl.pallas_call(kernel, out_shape=(jax.ShapeDtypeStruct((N, K), BF16), jax...  45.1 us
    pallas_call x1, Pallas kernels, body(): pl.pallas_call(finish, out_shape=(jax.ShapeDtypeStruct((N, K), BF16), jax...  1.13 us

profile of v4, /device:TPU:1, one launch (start us, length us, event | category | flops | bytes accessed | tf_op | source)
XLA Modules:
  0.0 47.6 jit_solution(17816271612417172480)
XLA Ops:
  1.3 45.1 %shard_map.121 = (bf16[1536,256]{1,0:T(8,128)(2,1)S(1)}, f32[2,256,256]{2,1,0:T(8,128)S(1)}) custom-call(bf16[1536,256]{1,0:T(8,128)(2,1)} %x_h.1, bf16[1536,256]{1,0:T(8,128)(2,1)} %res_h.1, s32[1,1536]{1,0:T(1,128)} %ord_h.1, bf16[1,1536,1536]{2,1,0:T(8,128)(2,1)} %diag_h.1, bf16[1,1536,128]{2,1,0:T(8,128)(2,1)} %up_h.1, bf16[1,1536,128]{2,1,0:T(8,128)(2,1)} %dn_h.1, ...), custom_call_target="tpu_custom_call" | custom-call | tf_op jit(solution)/shard_map/pallas_call | solution.py:281
  46.4 1.1 %shard_map.122 = (bf16[1536,256]{1,0:T(8,128)(2,1)}, f32[256,256]{1,0:T(8,128)}, f32[256,256]{1,0:T(8,128)}) custom-call(bf16[1536,256]{1,0:T(8,128)(2,1)S(1)} %get-tuple-element.5.image, f32[2,256,256]{2,1,0:T(8,128)S(1)} %get-tuple-element.6.grams), custom_call_target="tpu_custom_call" | custom-call | tf_op jit(solution)/shard_map/pallas_call | solution.py:290

commit v5 on v4

--- a/solution.py
+++ b/solution.py
@@ -29,7 +29,7 @@
     x_v, res_v, ord_v, diag_v, up_v, dn_v, lop_v, iop_v, w_v, path_v,
     p_v, pt_v, og_v, xt_v, loc_v, im_v,
     s0_v, sib_v, l1_v, a_r, root_v, b_r, t_v, u_v, q_v, vr_v, xv_v, c_v, c_r,
-    pre_v, gs_v, gs_r, h_v, h_r, z_v, z_r, f_v, f_r, o_r,
+    pre_v, ps_v, ps_r, po_v, xs_v, xs_r, h_v, h_r, z_v, z_r, f_v, f_r, o_r,
     load_sem, send_sem, recv_sem,
 ):
     me = lax.axis_index("leaf")
@@ -44,6 +44,12 @@
                    key=lambda s: -(min(s[0], 4 - s[0]) + min(s[1], 4 - s[1])))
     gy, gx = g // 4, lax.rem(g, 4)
     grp_peers = [lax.rem(gy + dy, 4) * 4 + lax.rem(gx + dx, 4) for dy, dx in steps]
+
+    def block_of(j):
+        return lax.rem(j, 2) * (D // 2) + j // 2
+
+    own_half = pl.ds(pl.multiple_of(core * R, R), R)
+    other_half = pl.ds(pl.multiple_of((1 - core) * R, R), R)
 
     def sib_of(a):
         return a + 1 - 2 * lax.rem(a, 2)
@@ -111,9 +117,9 @@
     pl.semaphore_wait(barrier, 2 * (D - 1))
 
     for j in leaf_peers:
-        remote(0, "leaf", l1_v.at[j], a_r.at[me], j).start()
+        remote(0, "leaf", l1_v.at[block_of(j)], a_r.at[me], j).start()
     remote(1, "leaf", s0_v, sib_v, sibling).start()
-    a_r[me] = l1_v[me]
+    a_r[me] = l1_v[block_of(me)]
 
     for t in range(3):
         rows = pl.ds(t * 512, 512)
@@ -159,6 +165,7 @@
         pt_v[j * R:(j + 1) * R, :] = jnp.where(row_high == jnp.asarray(j, BF16), row_one, jnp.zeros_like(row_one))
     l_dn.wait()
     vr_v[...] = mm(dn_v[...], lop_v[1]).astype(BF16)
+    xt_v[:K, :] = og_v[...].T
 
     arrived(0, a_r.at[0:15])
     s1 = [(a_r[2 * m].astype(F32) + a_r[2 * m + 1].astype(F32)).astype(BF16) for m in range(8)]
@@ -183,6 +190,10 @@
     arrived(1, sib_v)
     near = mmt(sib_v[...], lop_v[2]).astype(BF16)
     loc_v[...] = loc_v[...] + mmt(dn_v[...], near)
+    l_res.wait()
+    for t in range(3):
+        rows = pl.ds(t * 512, 512)
+        xt_v[K:, rows] = mm(p_v[rows, :], res_v[...]).astype(BF16).T
 
     arrived(2, b_r.at[0:15])
     c4 = mm(jnp.concatenate([b_r[j] for j in range(D)], axis=1), t_v[...].reshape(D * R, R)).astype(BF16)
@@ -191,34 +202,32 @@
         c_v[m] = (c1[m] + down[:, m * R:(m + 1) * R]).astype(BF16)
 
     for j in z_peers:
-        remote(3, "leaf", c_v.at[j // 2], c_r.at[z, core], j).start()
-    c_r[z, core] = c_v[z]
-
-    xt_v[:K, :] = og_v[...].T
-    l_res.wait()
-    for t in range(3):
-        rows = pl.ds(t * 512, 512)
-        xt_v[K:, rows] = mm(p_v[rows, :], res_v[...]).astype(BF16).T
+        remote(3, "leaf", c_v.at[j // 2], c_r.at[core, z], j).start()
+    c_r[core, z] = c_v[z]
+
     im_v[...] = loc_v[...].astype(BF16)
+    xv_v[...] = mm(xt_v[...], vr_v[...]).astype(BF16)
+    remote(10, "leaf", xv_v, xs_r, sibling).start()
     for t in range(2):
-        pre_v[t] = mm(xt_v[t * K:(t + 1) * K, :], im_v[...])
-    xv_v[...] = mm(xt_v[...], vr_v[...]).astype(BF16).reshape(2, K, R)
+        rows = pl.ds(t * K, K)
+        pre_v[rows, :] = mm(xt_v[rows, :], im_v[...])
+    ps_v[...] = pre_v[:, other_half].astype(BF16)
+    remote(5, "leaf", ps_v, ps_r, sibling).start()
+    arrived(10, xs_r)
+    xs_v[...] = (xv_v[...].astype(F32) + xs_r[...].astype(F32)).astype(BF16)
+    arrived(5, ps_r)
+    po_v[...] = pre_v[:, own_half] + ps_r[...].astype(F32)
 
     arrived(3, c_v.at[0:7])
-    remote(4, "leaf", c_r.at[:, core], c_r.at[:, core], sibling).start()
-    arrived(4, c_v)
-
-    coarse = c_r[...].reshape(K, R)
-    gs_v[...] = (pre_v[1 - core] + mmt(xv_v[1 - core], coarse)).astype(BF16)
-    remote(5, "leaf", gs_v, gs_r, sibling).start()
-    own = pre_v[core] + mmt(xv_v[core], coarse)
-    im_v[...] = (loc_v[...] + mmt(vr_v[...], coarse)).astype(BF16)
-    arrived(5, gs_r)
-    h_v[...] = (own + gs_r[...].astype(F32)).astype(BF16).reshape(D, C, K)
+    remote(4, "leaf", c_r.at[core], c_r.at[core], sibling).start()
+
+    h_v[...] = (po_v[...] + mmt(xs_v[...], c_r[core].reshape(R, R))).astype(BF16).reshape(D, 2 * C, R)
     for j in grp_peers:
         remote(6, "grp", h_v.at[j], h_r.at[g], j).start()
     h_r[g] = h_v[g]
 
+    arrived(4, c_v)
+    im_v[...] = (loc_v[...] + mmt(vr_v[...], c_r[...].reshape(K, R))).astype(BF16)
     for t in range(3):
         rows = pl.ds(t * 512, 512)
         img_v[rows, :] = mm(pt_v[rows, :], im_v[...]).astype(BF16)
@@ -242,11 +251,11 @@
     arrived(8, f_r.at[0:15])
     remote(9, "leaf", f_r, o_r, sibling).start()
     scale = 1.0 / (N * D * D)
-    out_v[core] = f_r[...].reshape(K, K).astype(F32) * scale
+    out_v[:, :, own_half] = (f_r[...].astype(F32) * scale).reshape(2, K, R)
     arrived(9, o_r)
-    out_v[1 - core] = o_r[...].reshape(K, K).astype(F32) * scale
+    out_v[:, :, other_half] = (o_r[...].astype(F32) * scale).reshape(2, K, R)
     for phase, ref in enumerate((
-        l1_v.at[0:15], s0_v, b_r.at[0:15], c_v.at[0:7], c_v, gs_v, h_v.at[0:15], z_r.at[0:7], f_r.at[0:15], f_r,
+        l1_v.at[0:15], s0_v, b_r.at[0:15], c_v.at[0:7], c_v, ps_v, h_v.at[0:15], z_r.at[0:7], f_r.at[0:15], f_r, xv_v,
     )):
         left(phase, ref)
 
@@ -272,10 +281,11 @@
         v((3, R, R), BF16), v((3, 14, R, R), BF16), v((28, R, R), BF16), v((7, R, R), BF16),
         v((N, N), BF16), v((N, N), BF16), v((N, K), BF16), v((2 * K, N), BF16), v((N, K), F32), v((N, K), BF16),
         v((K, R), BF16), v((K, R), BF16), v((D, C, R), BF16), v((D, C, R), BF16), v((C, R), BF16), v((D, C, R), BF16),
-        v((D, R, R), BF16), v((8 * R, R), BF16), v((8 * R, R), BF16), v((N, R), BF16), v((2, K, R), BF16), v((8, C, R), BF16), v((8, 2, C, R), BF16),
-        v((2, K, K), F32), v((K, K), BF16), v((K, K), BF16), v((D, C, K), BF16), v((D, C, K), BF16), v((C, K), BF16),
-        v((8, C, K), BF16), v((C, K), BF16), v((D, C, K), BF16), v((D, C, K), BF16),
-        dma((10,)), dma((10,)), dma((10,)),
+        v((D, R, R), BF16), v((8 * R, R), BF16), v((8 * R, R), BF16), v((N, R), BF16), v((2 * K, R), BF16), v((8, C, R), BF16), v((2, 8, C, R), BF16),
+        v((2 * K, K), F32), v((2 * K, R), BF16), v((2 * K, R), BF16), v((2 * K, R), F32), v((2 * K, R), BF16), v((2 * K, R), BF16),
+        v((D, 2 * C, R), BF16), v((D, 2 * C, R), BF16), v((2 * C, R), BF16), v((8, 2 * C, R), BF16), v((2 * C, R), BF16),
+        v((D, 2 * C, R), BF16), v((D, 2 * C, R), BF16),
+        dma((10,)), dma((11,)), dma((11,)),
     ]
     args = [pltpu.with_memory_space_constraint(a, pltpu.HBM) for a in args[:-1]] + [args[-1]]
     image, grams = pl.pallas_call(

time: 47.7 us -> 44.9 us (0.941)
  Pallas kernels: 46.3 us -> 43.5 us
    pallas_call x1, Pallas kernels: 45.1 us -> 42.4 us  [body(): pl.pallas_call(kernel, out_shape=(jax.ShapeDtypeStruct((N, K), BF16), jax...]
where the time goes in v5:
time: 44.9 us; the launch traced here: 44.8 us
  Pallas kernels  43.5 us (97%)
  between operations  1.29 us (3%)
    pallas_call x1, Pallas kernels, body(): pl.pallas_call(kernel, out_shape=(jax.ShapeDtypeStruct((N, K), BF16), jax...  42.4 us
    pallas_call x1, Pallas kernels, body(): pl.pallas_call(finish, out_shape=(jax.ShapeDtypeStruct((N, K), BF16), jax...  1.13 us

profile of v5, /device:TPU:1, one launch (start us, length us, event | category | flops | bytes accessed | tf_op | source)
XLA Modules:
  0.0 44.8 jit_solution(7431170574957861641)
XLA Ops:
  1.3 42.4 %shard_map.121 = (bf16[1536,256]{1,0:T(8,128)(2,1)S(1)}, f32[2,256,256]{2,1,0:T(8,128)S(1)}) custom-call(bf16[1536,256]{1,0:T(8,128)(2,1)} %x_h.1, bf16[1536,256]{1,0:T(8,128)(2,1)} %res_h.1, s32[1,1536]{1,0:T(1,128)} %ord_h.1, bf16[1,1536,1536]{2,1,0:T(8,128)(2,1)} %diag_h.1, bf16[1,1536,128]{2,1,0:T(8,128)(2,1)} %up_h.1, bf16[1,1536,128]{2,1,0:T(8,128)(2,1)} %dn_h.1, ...), custom_call_target="tpu_custom_call" | custom-call | tf_op jit(solution)/shard_map/pallas_call | solution.py:291
  43.7 1.1 %shard_map.122 = (bf16[1536,256]{1,0:T(8,128)(2,1)}, f32[256,256]{1,0:T(8,128)}, f32[256,256]{1,0:T(8,128)}) custom-call(bf16[1536,256]{1,0:T(8,128)(2,1)S(1)} %get-tuple-element.5.image, f32[2,256,256]{2,1,0:T(8,128)S(1)} %get-tuple-element.6.grams), custom_call_target="tpu_custom_call" | custom-call | tf_op jit(solution)/shard_map/pallas_call | solution.py:300

commit v6 on v5

--- a/solution.py
+++ b/solution.py
@@ -247,9 +247,12 @@
     f_v[...] = total.astype(BF16)
     for j in grp_peers:
         remote(8, "grp", f_v, f_r.at[g], j).start()
+        pltpu.make_async_remote_copy(
+            src_ref=f_v, dst_ref=o_r.at[g], send_sem=send_sem.at[9], recv_sem=recv_sem.at[9],
+            device_id={"grp": j, "leaf": sibling}, device_id_type=pl.DeviceIdType.MESH).start()
+    remote(9, "leaf", f_v, o_r.at[g], sibling).start()
     f_r[g] = f_v[...]
     arrived(8, f_r.at[0:15])
-    remote(9, "leaf", f_r, o_r, sibling).start()
     scale = 1.0 / (N * D * D)
     out_v[:, :, own_half] = (f_r[...].astype(F32) * scale).reshape(2, K, R)
     arrived(9, o_r)

time: 44.9 us -> 44.1 us (0.982)
  Pallas kernels: 43.5 us -> 42.7 us
    pallas_call x1, Pallas kernels: 42.4 us -> 41.6 us  [body(): pl.pallas_call(kernel, out_shape=(jax.ShapeDtypeStruct((N, K), BF16), jax...]
where the time goes in v6:
time: 44.1 us; the launch traced here: 44 us
  Pallas kernels  42.7 us (97%)
  between operations  1.29 us (3%)
    pallas_call x1, Pallas kernels, body(): pl.pallas_call(kernel, out_shape=(jax.ShapeDtypeStruct((N, K), BF16), jax...  41.6 us
    pallas_call x1, Pallas kernels, body(): pl.pallas_call(finish, out_shape=(jax.ShapeDtypeStruct((N, K), BF16), jax...  1.13 us

profile of v6, /device:TPU:1, one launch (start us, length us, event | category | flops | bytes accessed | tf_op | source)
XLA Modules:
  0.0 44.0 jit_solution(9507938112131217895)
XLA Ops:
  1.3 41.6 %shard_map.121 = (bf16[1536,256]{1,0:T(8,128)(2,1)S(1)}, f32[2,256,256]{2,1,0:T(8,128)S(1)}) custom-call(bf16[1536,256]{1,0:T(8,128)(2,1)} %x_h.1, bf16[1536,256]{1,0:T(8,128)(2,1)} %res_h.1, s32[1,1536]{1,0:T(1,128)} %ord_h.1, bf16[1,1536,1536]{2,1,0:T(8,128)(2,1)} %diag_h.1, bf16[1,1536,128]{2,1,0:T(8,128)(2,1)} %up_h.1, bf16[1,1536,128]{2,1,0:T(8,128)(2,1)} %dn_h.1, ...), custom_call_target="tpu_custom_call" | custom-call | tf_op jit(solution)/shard_map/pallas_call | solution.py:294
  42.9 1.1 %shard_map.122 = (bf16[1536,256]{1,0:T(8,128)(2,1)}, f32[256,256]{1,0:T(8,128)}, f32[256,256]{1,0:T(8,128)}) custom-call(bf16[1536,256]{1,0:T(8,128)(2,1)S(1)} %get-tuple-element.5.image, f32[2,256,256]{2,1,0:T(8,128)S(1)} %get-tuple-element.6.grams), custom_call_target="tpu_custom_call" | custom-call | tf_op jit(solution)/shard_map/pallas_call | solution.py:303
